TPU v7x, 32 devices: a whole 2x2x4 slice. The times are simulated.
32 devices in a mesh: lat: 4 (over y, x), lon: 8 (over z, core).
Axes of the slice: x: 2, y: 2, z: 4, core: 2. Of those that a mesh axis runs over, the one named last changes fastest.
Arguments:
- members: float32 [80, 2, 256, 1024], P('lon', None, 'lat'), may hold values from -6 to 6
- obs_row: int32 [2, 4, 8, 64], P(None, 'lat', 'lon'), may hold values from 0 to 63
- obs_col: int32 [2, 4, 8, 64], P(None, 'lat', 'lon'), may hold values from 0 to 127
- obs_value: float32 [2, 4, 8, 64], P(None, 'lat', 'lon'), may hold values from -6 to 6
- obs_error: float32 [2, 4, 8, 64], P(None, 'lat', 'lon'), may hold values from 0.25 to 4
- obs_weight: float32 [2, 4, 8, 2, 64], P(None, 'lat', 'lon'), may hold values from 0.2 to 1
- obs_count: int32 [2, 4, 8], P(None, 'lat', 'lon'), may hold values from 8 to 64, as said below
Outputs:
- analysis: float32 [80, 2, 256, 1024], P('lon', None, 'lat')
Inputs may be any that keep to these rules, and one draw needn't show every extreme that they name: The first obs_count slots of a tile hold its observations, the others are ignored; in each batch one tile holds 64. `obs_row`: row inside the owning tile. `obs_col`: column inside the owning tile.
All inputs are finite; a program needn't handle non-finite values.
Results may differ from a plain program's by a relative error of at most 0.0001.
Values sent between devices are 32-bit elements; how exact they have to be, the bound alone decides.
A program may use at most 192 MiB of HBM per device.

v0:
```python
import math

import jax
import jax.numpy as jnp
from jax import lax
from jax.sharding import PartitionSpec as P

NBATCH = 2
RAD = 48


def extended(block, sides, width):
    for axis, dim in sides:
        count = lax.axis_size(axis)
        forward = [(i, i + 1) for i in range(count - 1)]
        forward.append((count - 1, 0))
        backward = [(target, source) for source, target in forward]
        low = lax.ppermute(
            lax.slice_in_dim(block, block.shape[dim] - width, None, axis=dim), axis, forward
        )
        high = lax.ppermute(lax.slice_in_dim(block, 0, width, axis=dim), axis, backward)
        block = jnp.concatenate([low, block, high], axis=dim)
    return block


def gaspari(dist):
    z = dist / (0.5 * RAD)
    near = (((-0.25 * z + 0.5) * z + 0.625) * z - 5.0 / 3.0) * z * z + 1.0
    zfar = jnp.maximum(z, 1.0)
    far = (
        ((((zfar / 12.0 - 0.5) * zfar + 0.625) * zfar + 5.0 / 3.0) * zfar - 5.0) * zfar
        + 4.0
        - 2.0 / (3.0 * zfar)
    )
    return jnp.where(z <= 1.0, near, jnp.where(z < 2.0, far, 0.0))


def body(members, obs_row, obs_col, obs_value, obs_error, obs_weight, obs_count):
    lon_parts = lax.axis_size("lon")
    group = members.shape[0]
    full = group * lon_parts
    clat = members.shape[2]
    nlon = members.shape[3]
    clon = nlon // lon_parts
    slot_count = obs_row.shape[-1]
    lat_first = lax.axis_index("lat") * clat
    lon_first = lax.axis_index("lon") * clon
    highest = lax.Precision.HIGHEST
    state = lax.all_to_all(members, "lon", split_axis=3, concat_axis=0, tiled=True)
    first_left = 0
    for batch in range(first_left, NBATCH):
        picked = state[:, :, obs_row[batch, 0, 0], obs_col[batch, 0, 0]]
        prior = jnp.einsum("klo,lo->ko", picked, obs_weight[batch, 0, 0], precision=highest)
        valid = (jnp.arange(slot_count) < obs_count[batch, 0, 0]).astype(jnp.float32)
        prior_mean = jnp.mean(prior, axis=0)
        summarize_prior_pert = prior - prior_mean
        spread = jnp.sum(summarize_prior_pert * summarize_prior_pert, axis=0) / (full - 1.0)
        err = obs_error[batch, 0, 0]
        denom = spread + err
        summarize_mean_coef = valid * (obs_value[batch, 0, 0] - prior_mean) / denom
        summarize_pert_coef = valid / (denom * (1.0 + jnp.sqrt(err / denom)))
        glat = (lat_first + obs_row[batch, 0, 0]).astype(jnp.float32)
        glon = (lon_first + obs_col[batch, 0, 0]).astype(jnp.float32)
        extra = jnp.stack([summarize_mean_coef, summarize_pert_coef, glat, glon], axis=0)
        packed = jnp.concatenate([summarize_prior_pert, extra], axis=0)
        wide = extended(packed[:, None, None, :], (("lat", 1), ("lon", 2)), 1)
        received = wide.reshape(packed.shape[0], -1)
        members_here = state.shape[0]
        levels = state.shape[1]
        mean = jnp.mean(state, axis=0)
        pert = state - mean
        prior_pert = received[:members_here]
        mean_coef = received[members_here]
        pert_coef = received[members_here + 1]
        obs_lat = received[members_here + 2]
        obs_lon = received[members_here + 3]
        coef = mean_coef[:, None] - pert_coef[:, None] * prior_pert.T
        rows_block = math.gcd(clat, max(1, 2048 // clon))
        block_count = clat // rows_block
        cells = rows_block * clon
        blocks = jnp.moveaxis(pert.reshape(members_here, levels, block_count, cells), 2, 0)
        half = 0.5 * nlon

        def one_block(item):
            block, which = item
            local = jnp.arange(cells)
            cell_lat = (lat_first + which * rows_block + local // clon).astype(jnp.float32)
            cell_lon = (lon_first + local % clon).astype(jnp.float32)
            delta_lat = cell_lat[:, None] - obs_lat[None, :]
            delta_lon = jnp.mod(cell_lon[:, None] - obs_lon[None, :] + half, 1.0 * nlon) - half
            taper = gaspari(jnp.sqrt(delta_lat * delta_lat + delta_lon * delta_lon))
            cov = jnp.einsum("kpc,km->pcm", block, prior_pert, precision=highest) / (
                members_here - 1.0
            )
            return jnp.einsum("pcm,mk->kpc", cov * taper[None], coef, precision=highest)

        increments = lax.map(one_block, (blocks, jnp.arange(block_count)))
        state = state + jnp.moveaxis(increments, 0, 2).reshape(state.shape)
    return lax.all_to_all(state, "lon", split_axis=0, concat_axis=3, tiled=True)


def solution(mesh):
    placed = (
        P("lon", None, "lat", None),
        P(None, "lat", "lon", None),
        P(None, "lat", "lon", None),
        P(None, "lat", "lon", None),
        P(None, "lat", "lon", None),
        P(None, "lat", "lon", None, None),
        P(None, "lat", "lon"),
    )
    return jax.shard_map(
        body, mesh=mesh, in_specs=placed, out_specs=P("lon", None, "lat", None), check_vma=False
    )
```

profile of v0, /device:TPU:0, one launch (start us, length us, event | category | flops | bytes accessed | tf_op | source)
XLA Modules:
  0.0 839.3 jit_solution(459850053425190709)
XLA Ops:
  0.0 14.7 %copy.109 = f32[10,2,64,1024]{2,0,1,3:T(8,128)} copy(f32[10,2,64,1024]{3,2,1,0:T(8,128)} %param.11) | data formatting | bytes 10485760 | tf_op args[0]
  14.7 12.8 %reshape.700 = f32[8,1,163840]{2,1,0:T(1,128)} reshape(f32[1024,2,10,64]{3,2,1,0:T(8,128)} %bitcast.193) | data formatting | bytes 10485760
  27.5 6.5 all-to-all-start
  35.3 115.3 %all-to-all-done = f32[8,1,163840]{2,1,0:T(1,128)} async-done(((f32[8,1,163840]{2,1,0:T(1,128)}), f32[8,1,163840]{2,1,0:T(1,128)}, u32[]{:S(2)}, u32[]{:S(2)}) %all-to-all-start) | async-done | bytes 5242912 | tf_op jit(solution)/shard_map/all_to_all | solution.py:49
  151.2 16.6 %reduce.24 = f32[8,163840]{1,0:T(8,128)} reduce(f32[8,1,163840]{2,1,0:T(1,128)} %all-to-all-done, f32[]{:T(128)} %broadcast.1090), dimensions={1}, to_apply=%all_to_all.28.reduce_sub_computation | reduce | bytes 10485764 | tf_op jit(solution)/shard_map/all_to_all | solution.py:49
  167.8 13.2 %reshape.701 = f32[1024,2,10,64]{3,2,1,0:T(8,128)} reshape(f32[8,163840]{1,0:T(8,128)} %reduce.24) | data formatting | bytes 10485760
  181.0 12.2 %copy.111 = f32[8,10,2,64,128]{4,3,2,1,0:T(8,128)} copy(f32[8,10,2,64,128]{3,1,2,4,0:T(8,128)} %bitcast.190) | data formatting | bytes 10485760 | tf_op jit(solution)/shard_map/all_to_all | solution.py:49
  193.1 8.8 %copy.113 = f32[80,2,64,128]{0,1,3,2:T(2,128)} copy(f32[80,2,64,128]{3,2,1,0:T(8,128)} %bitcast.192) | data formatting | bytes 10485760 | tf_op jit(solution)/shard_map/all_to_all | solution.py:49
  201.9 4.1 gather_fusion
  211.2 10.3 %copy.137 = f32[10,2,64,8,128]{4,3,2,1,0:T(8,128)} copy(f32[10,2,64,8,128]{2,0,1,4,3:T(8,128)} %bitcast.191) | data formatting | bytes 10485760 | tf_op jit(solution)/shard_map/all_to_all | solution.py:49
  224.3 7.3 all_to_all.32
  231.7 3.5 collective-permute-start.3
  235.2 7.2 subtract_bitcast_fusion.1
  244.0 246.9 %while.24 = (s32[]{:T(128)}, f32[4,80,2,2048]{3,0,2,1:T(4,128)}, f32[4,80,2,2048]{3,0,2,1:T(4,128)}, f32[80,576]{1,0:T(8,128)S(1)}, s32[4]{0:T(128)S(1)}, /*inde...) while((s32[]{:T(128)}, f32[4,80,2,2048]{3,0,2,1:T(4,128)}, ...), condition=%wide.region_4.5_spmd, body=%wide.region_3.4_spmd.sunk | while | flops 4581785600 | bytes 39212736 | solution.py:97
  263.7 9.7 %fusion.114 = f32[2048,576]{0,1:T(8,128)S(1)} fusion(f32[576]{0:T(1024)S(1)} %reduce.29, f32[2048]{0:T(1024)S(1)} %get-tuple-element.559, f32[576]{0:T(1024)S(1)} %reduce.30, f32[2048]{0:T(1024)S(1)} %get-tuple-element.560), kind=kLoop, calls=%fused_computation.12.clone.1 | loop fusion | flops 49545216 | bytes 4739584 | tf_op jit(solution)/shard_map/while/body/eval_jaxpr/mul | solution.py:95
  273.3 3.9 constant_dynamic-slice_fusion.4
  277.2 7.8 fusion.112
  285.1 6.8 fusion.115
  293.2 24.1 %dynamic_update_slice.16 = f32[4,80,2,2048]{3,0,2,1:T(4,128)} dynamic-update-slice(f32[4,80,2,2048]{3,0,2,1:T(4,128)} %get-tuple-element.588, f32[1,80,2,2048]{3,0,2,1:T(1,128)S(1)} %copy.162, s32[]{:T(128)} %get-tuple-element.587, s32[]{:T(128)} %constant.329.clone.1..sunk, s32[]{:T(128)} %constant.329.clone.1..sunk, s32[]{:T(128)} %constant.329.clone.1..sunk) | dynamic-update-slice | bytes 2621444 | tf_op jit(solution)/shard_map/while/body/jit(dynamic_update_index_in_dim)/dynamic_update_slice | solution.py:97
  318.7 9.7 %fusion.114 = f32[2048,576]{0,1:T(8,128)S(1)} fusion(f32[576]{0:T(1024)S(1)} %reduce.29, f32[2048]{0:T(1024)S(1)} %get-tuple-element.559, f32[576]{0:T(1024)S(1)} %reduce.30, f32[2048]{0:T(1024)S(1)} %get-tuple-element.560), kind=kLoop, calls=%fused_computation.12.clone.1 | loop fusion | flops 49545216 | bytes 4739584 | tf_op jit(solution)/shard_map/while/body/eval_jaxpr/mul | solution.py:95
  328.3 3.9 constant_dynamic-slice_fusion.4
  332.3 7.8 fusion.112
  340.1 6.8 fusion.115
  348.3 24.1 %dynamic_update_slice.16 = f32[4,80,2,2048]{3,0,2,1:T(4,128)} dynamic-update-slice(f32[4,80,2,2048]{3,0,2,1:T(4,128)} %get-tuple-element.588, f32[1,80,2,2048]{3,0,2,1:T(1,128)S(1)} %copy.162, s32[]{:T(128)} %get-tuple-element.587, s32[]{:T(128)} %constant.329.clone.1..sunk, s32[]{:T(128)} %constant.329.clone.1..sunk, s32[]{:T(128)} %constant.329.clone.1..sunk) | dynamic-update-slice | bytes 2621444 | tf_op jit(solution)/shard_map/while/body/jit(dynamic_update_index_in_dim)/dynamic_update_slice | solution.py:97
  373.7 9.7 %fusion.114 = f32[2048,576]{0,1:T(8,128)S(1)} fusion(f32[576]{0:T(1024)S(1)} %reduce.29, f32[2048]{0:T(1024)S(1)} %get-tuple-element.559, f32[576]{0:T(1024)S(1)} %reduce.30, f32[2048]{0:T(1024)S(1)} %get-tuple-element.560), kind=kLoop, calls=%fused_computation.12.clone.1 | loop fusion | flops 49545216 | bytes 4739584 | tf_op jit(solution)/shard_map/while/body/eval_jaxpr/mul | solution.py:95
  383.4 3.9 constant_dynamic-slice_fusion.4
  387.3 7.8 fusion.112
  395.1 6.8 fusion.115
  403.3 24.1 %dynamic_update_slice.16 = f32[4,80,2,2048]{3,0,2,1:T(4,128)} dynamic-update-slice(f32[4,80,2,2048]{3,0,2,1:T(4,128)} %get-tuple-element.588, f32[1,80,2,2048]{3,0,2,1:T(1,128)S(1)} %copy.162, s32[]{:T(128)} %get-tuple-element.587, s32[]{:T(128)} %constant.329.clone.1..sunk, s32[]{:T(128)} %constant.329.clone.1..sunk, s32[]{:T(128)} %constant.329.clone.1..sunk) | dynamic-update-slice | bytes 2621444 | tf_op jit(solution)/shard_map/while/body/jit(dynamic_update_index_in_dim)/dynamic_update_slice | solution.py:97
  428.7 9.7 %fusion.114 = f32[2048,576]{0,1:T(8,128)S(1)} fusion(f32[576]{0:T(1024)S(1)} %reduce.29, f32[2048]{0:T(1024)S(1)} %get-tuple-element.559, f32[576]{0:T(1024)S(1)} %reduce.30, f32[2048]{0:T(1024)S(1)} %get-tuple-element.560), kind=kLoop, calls=%fused_computation.12.clone.1 | loop fusion | flops 49545216 | bytes 4739584 | tf_op jit(solution)/shard_map/while/body/eval_jaxpr/mul | solution.py:95
  438.4 3.9 constant_dynamic-slice_fusion.4
  442.3 7.8 fusion.112
  450.1 6.8 fusion.115
  458.3 24.1 %dynamic_update_slice.16 = f32[4,80,2,2048]{3,0,2,1:T(4,128)} dynamic-update-slice(f32[4,80,2,2048]{3,0,2,1:T(4,128)} %get-tuple-element.588, f32[1,80,2,2048]{3,0,2,1:T(1,128)S(1)} %copy.162, s32[]{:T(128)} %get-tuple-element.587, s32[]{:T(128)} %constant.329.clone.1..sunk, s32[]{:T(128)} %constant.329.clone.1..sunk, s32[]{:T(128)} %constant.329.clone.1..sunk) | dynamic-update-slice | bytes 2621444 | tf_op jit(solution)/shard_map/while/body/jit(dynamic_update_index_in_dim)/dynamic_update_slice | solution.py:97
  490.9 7.7 reshape.665
  498.6 8.1 bitcast_add_fusion.3
  506.8 8.8 %copy.123 = f32[80,2,64,128]{0,1,3,2:T(2,128)} copy(f32[80,2,64,128]{3,2,1,0:T(8,128)} %bitcast_add_fusion.3) | data formatting | bytes 10485760 | tf_op jit(solution)/shard_map/add | solution.py:98
  515.5 4.1 gather_fusion.1
  524.5 7.7 reshape.666
  532.2 7.9 fusion.71
  540.3 3.5 collective-permute-start.7
  543.8 10.1 %subtract_bitcast_fusion = f32[4,80,2,2048]{3,0,2,1:T(4,128)} fusion(f32[80,2,4,2048]{3,2,1,0:T(4,128)} %all_to_all.32, f32[2,4,2048]{2,1,0:T(4,128)S(1)} %div.148, f32[4,80,2,2048]{3,0,2,1:T(4,128)} %get-tuple-element.271), kind=kLoop, calls=%fused_computation.99 | loop fusion | flops 2621440 | bytes 15794176 | tf_op jit(solution)/shard_map/transpose | solution.py:81
  555.5 140.1 %while.25 = (s32[]{:T(128)}, f32[4,80,2,2048]{3,1,2,0:T(8,128)}, f32[4,80,2,2048]{3,0,2,1:T(4,128)}, f32[80,576]{1,0:T(8,128)S(1)}, s32[4]{0:T(128)S(1)}, /*inde...) while((s32[]{:T(128)}, f32[4,80,2,2048]{3,1,2,0:T(8,128)}, ...), condition=%wide.region_9.10_spmd, body=%wide.region_8.9_spmd.sunk | while | flops 4581785600 | bytes 33970356 | solution.py:97
  574.0 9.7 %fusion.121 = f32[2048,576]{0,1:T(8,128)S(1)} fusion(f32[576]{0:T(1024)S(1)} %reduce.31, f32[2048]{0:T(1024)S(1)} %get-tuple-element.571, f32[576]{0:T(1024)S(1)} %reduce.32, f32[2048]{0:T(1024)S(1)} %get-tuple-element.572), kind=kLoop, calls=%fused_computation.58.clone.1 | loop fusion | flops 49545216 | bytes 4739584 | tf_op jit(solution)/shard_map/while/body/eval_jaxpr/mul | solution.py:95
  583.7 3.9 constant_dynamic-slice_fusion.5
  587.6 7.9 fusion.119
  595.5 8.0 fusion.122
  604.8 9.7 %fusion.121 = f32[2048,576]{0,1:T(8,128)S(1)} fusion(f32[576]{0:T(1024)S(1)} %reduce.31, f32[2048]{0:T(1024)S(1)} %get-tuple-element.571, f32[576]{0:T(1024)S(1)} %reduce.32, f32[2048]{0:T(1024)S(1)} %get-tuple-element.572), kind=kLoop, calls=%fused_computation.58.clone.1 | loop fusion | flops 49545216 | bytes 4739584 | tf_op jit(solution)/shard_map/while/body/eval_jaxpr/mul | solution.py:95
  614.4 3.9 constant_dynamic-slice_fusion.5
  618.3 7.9 fusion.119
  626.2 7.9 fusion.122
  635.4 9.7 %fusion.121 = f32[2048,576]{0,1:T(8,128)S(1)} fusion(f32[576]{0:T(1024)S(1)} %reduce.31, f32[2048]{0:T(1024)S(1)} %get-tuple-element.571, f32[576]{0:T(1024)S(1)} %reduce.32, f32[2048]{0:T(1024)S(1)} %get-tuple-element.572), kind=kLoop, calls=%fused_computation.58.clone.1 | loop fusion | flops 49545216 | bytes 4739584 | tf_op jit(solution)/shard_map/while/body/eval_jaxpr/mul | solution.py:95
  645.1 3.9 constant_dynamic-slice_fusion.5
  649.0 7.9 fusion.119
  656.8 7.9 fusion.122
  666.0 9.7 %fusion.121 = f32[2048,576]{0,1:T(8,128)S(1)} fusion(f32[576]{0:T(1024)S(1)} %reduce.31, f32[2048]{0:T(1024)S(1)} %get-tuple-element.571, f32[576]{0:T(1024)S(1)} %reduce.32, f32[2048]{0:T(1024)S(1)} %get-tuple-element.572), kind=kLoop, calls=%fused_computation.58.clone.1 | loop fusion | flops 49545216 | bytes 4739584 | tf_op jit(solution)/shard_map/while/body/eval_jaxpr/mul | solution.py:95
  675.7 3.9 constant_dynamic-slice_fusion.5
  679.6 7.9 fusion.119
  687.5 7.9 fusion.122
  695.6 8.2 copy.131
  703.8 7.7 reshape.667
  711.5 5.3 add.533
  716.8 119.1 %all_to_all.39 = f32[80,2,64,128]{3,2,1,0:T(8,128)S(1)} all-to-all(f32[80,2,64,128]{3,2,1,0:T(8,128)S(1)} %add.533), channel_id=1, replica_groups=mesh['lat'=4,'lon'=8] {'lon'}, dimensions={0} | all-to-all | bytes 10485760 | tf_op jit(solution)/shard_map/all_to_all | solution.py:99
  835.8 3.1 copy.157
  (119 shorter events, 28.5 us)
Async XLA Ops:
  27.5 6.5 copy-start.2
  27.5 6.6 copy-start.1
  27.5 6.7 copy-start
  27.5 7.1 copy-start.3
  27.5 123.1 %all-to-all-start = ((f32[8,1,163840]{2,1,0:T(1,128)}), f32[8,1,163840]{2,1,0:T(1,128)}, u32[]{:S(2)}, u32[]{:S(2)}) async-start(f32[8,1,163840]{2,1,0:T(1,128)} %reshape.700), calls=%async_computation | async-start | bytes 10485760 | tf_op jit(solution)/shard_map/all_to_all | solution.py:49
  193.1 13.8 %copy-start.4 = (f32[2,1,1,64]{3,2,1,0:T(1,128)S(1)}, f32[2,1,1,64]{3,2,1,0:T(1,128)}, u32[]{:S(2)}) copy-start(f32[2,1,1,64]{3,2,1,0:T(1,128)} %param.15) | copy-start | bytes 1540
  193.1 13.8 %copy-start.5 = (f32[2,1,1,64]{3,2,1,0:T(1,128)S(1)}, f32[2,1,1,64]{3,2,1,0:T(1,128)}, u32[]{:S(2)}) copy-start(f32[2,1,1,64]{3,2,1,0:T(1,128)} %param.14) | copy-start | bytes 1540
  207.9 23.6 %collective-permute-start = (f32[84,1,1,64]{0,3,2,1:T(8,128)S(1)}, f32[84,1,1,64]{0,3,2,1:T(8,128)S(1)}, u32[]{:S(2)}, u32[]{:S(2)}) collective-permute-start(f32[84,1,1,64]{0,3,2,1:T(8,128)S(1)} %bitcast.205), channel_id=1, source_target_pairs={{0,8},{8,16},{16,24},{24,0},{1,9},{9,17},{17,25},{25,1},{2,10},{10... | collective-permute-start | bytes 64520 | tf_op jit(solution)/shard_map/ppermute | solution.py:18
  209.5 22.1 %collective-permute-start.1 = (f32[84,1,1,64]{0,3,2,1:T(8,128)S(1)}, f32[84,1,1,64]{0,3,2,1:T(8,128)S(1)}, u32[]{:S(2)}, u32[]{:S(2)}) collective-permute-start(f32[84,1,1,64]{0,3,2,1:T(8,128)S(1)} %bitcast.206), channel_id=1, source_target_pairs={{8,0},{16,8},{24,16},{0,24},{9,1},{17,9},{25,17},{1,25},{10,2},{18... | collective-permute-start | bytes 64520 | tf_op jit(solution)/shard_map/ppermute | solution.py:21
  231.6 10.8 %collective-permute-start.2 = (f32[84,3,1,64]{0,3,2,1:T(8,128)S(1)}, f32[84,3,1,64]{0,3,2,1:T(8,128)S(1)}, u32[]{:S(2)}, u32[]{:S(2)}) collective-permute-start(f32[84,3,1,64]{0,3,2,1:T(8,128)S(1)} %pad_maximum_fusion.2), channel_id=1, source_target_pairs={{0,1},{1,2},{2,3},{3,4},{4,5},{5,6},{6,7},{7,0},{8,9},{9,10},{10,1... | collective-permute-start | bytes 193544 | tf_op jit(solution)/shard_map/ppermute | solution.py:18
  231.7 10.7 %collective-permute-start.3 = (f32[84,3,1,64]{0,3,2,1:T(8,128)S(1)}, f32[84,3,1,64]{0,3,2,1:T(8,128)S(1)}, u32[]{:S(2)}, u32[]{:S(2)}) collective-permute-start(f32[84,3,1,64]{0,3,2,1:T(8,128)S(1)} %pad_maximum_fusion.2), channel_id=1, source_target_pairs={{1,0},{2,1},{3,2},{4,3},{5,4},{6,5},{7,6},{0,7},{9,8},{10,9},{11,1... | collective-permute-start | bytes 193544 | tf_op jit(solution)/shard_map/ppermute | solution.py:21
  521.5 18.7 %collective-permute-start.4 = (f32[84,1,1,64]{0,3,2,1:T(8,128)S(1)}, f32[84,1,1,64]{0,3,2,1:T(8,128)S(1)}, u32[]{:S(2)}, u32[]{:S(2)}) collective-permute-start(f32[84,1,1,64]{0,3,2,1:T(8,128)S(1)} %bitcast.201), channel_id=1, source_target_pairs={{0,8},{8,16},{16,24},{24,0},{1,9},{9,17},{17,25},{25,1},{2,10},{10... | collective-permute-start | bytes 64520 | tf_op jit(solution)/shard_map/ppermute | solution.py:18
  522.2 18.0 %collective-permute-start.5 = (f32[84,1,1,64]{0,3,2,1:T(8,128)S(1)}, f32[84,1,1,64]{0,3,2,1:T(8,128)S(1)}, u32[]{:S(2)}, u32[]{:S(2)}) collective-permute-start(f32[84,1,1,64]{0,3,2,1:T(8,128)S(1)} %bitcast.202), channel_id=1, source_target_pairs={{8,0},{16,8},{24,16},{0,24},{9,1},{17,9},{25,17},{1,25},{10,2},{18... | collective-permute-start | bytes 64520 | tf_op jit(solution)/shard_map/ppermute | solution.py:21
  540.2 13.7 %collective-permute-start.6 = (f32[84,3,1,64]{0,3,2,1:T(8,128)S(1)}, f32[84,3,1,64]{0,3,2,1:T(8,128)S(1)}, u32[]{:S(2)}, u32[]{:S(2)}) collective-permute-start(f32[84,3,1,64]{0,3,2,1:T(8,128)S(1)} %pad_maximum_fusion.3), channel_id=1, source_target_pairs={{0,1},{1,2},{2,3},{3,4},{4,5},{5,6},{6,7},{7,0},{8,9},{9,10},{10,1... | collective-permute-start | bytes 193544 | tf_op jit(solution)/shard_map/ppermute | solution.py:18
  540.3 13.6 %collective-permute-start.7 = (f32[84,3,1,64]{0,3,2,1:T(8,128)S(1)}, f32[84,3,1,64]{0,3,2,1:T(8,128)S(1)}, u32[]{:S(2)}, u32[]{:S(2)}) collective-permute-start(f32[84,3,1,64]{0,3,2,1:T(8,128)S(1)} %pad_maximum_fusion.3), channel_id=1, source_target_pairs={{1,0},{2,1},{3,2},{4,3},{5,4},{6,5},{7,6},{0,7},{9,8},{10,9},{11,1... | collective-permute-start | bytes 193544 | tf_op jit(solution)/shard_map/ppermute | solution.py:21
where the time goes:
time: 852 us; the launch traced here: 839 us
  local copies, waits for them, and re-layouts  274 us (32%)
  other arithmetic  138 us (16%)
  matrix products  123 us (14%)
  blocking collectives  119 us (14%)
  waiting for transfers between devices  115 us (13%)
  loops' own time  49.7 us (6%)
  starting transfers between devices  19.8 us (2%)
    all_to_all x1, blocking collectives, body(): return lax.all_to_all(state, 'lon', split_axis=0, concat_axis=3, tiled=True)  119 us
    all_to_all x1, waiting for transfers between devices, body(): lax.all_to_all(members, 'lon', split_axis=3, concat_axis=0, tiled=True)  115 us
    dynamic_update_slice x8, local copies, waits for them, and re-layouts, body(): increments = lax.map(one_block, (blocks, jnp.arange(block_count)))  102 us
    mul x8, other arithmetic, one_block(): return jnp.einsum('pcm,mk->kpc', cov * taper[None], coef, precision=highest)  77.2 us
    dot_general x8, matrix products, one_block(): jnp.einsum('kpc,km->pcm', block, prior_pert, precision=highest)  62.8 us
    dot_general x8, matrix products, one_block(): return jnp.einsum('pcm,mk->kpc', cov * taper[None], coef, precision=highest)  58.8 us
    another operation x2, loops' own time, body(): increments = lax.map(one_block, (blocks, jnp.arange(block_count)))  49.7 us
    unnamed x15, local copies, waits for them, and re-layouts  40.7 us
  transfers between devices with their start and end apart: 9, of which 1 were waited for; matrix products, arithmetic and copies ran while one was open for 6% of the time, Pallas kernels for 0%

commit v1 on v0

v1 whole, which is shorter than its diff:
```python
import functools

import jax
import jax.numpy as jnp
from jax import lax
from jax.experimental import pallas as pl
from jax.experimental.pallas import tpu as pltpu
from jax.sharding import PartitionSpec as P

NBATCH = 2
RAD = 48
CHUNKS = 4
HIGHEST = lax.Precision.HIGHEST


def extended(block, sides, width):
    for axis, dim in sides:
        count = lax.axis_size(axis)
        forward = [(i, (i + 1) % count) for i in range(count)]
        backward = [(target, source) for source, target in forward]
        low = lax.ppermute(
            lax.slice_in_dim(block, block.shape[dim] - width, None, axis=dim), axis, forward
        )
        high = lax.ppermute(lax.slice_in_dim(block, 0, width, axis=dim), axis, backward)
        block = jnp.concatenate([low, block, high], axis=dim)
    return block


def gaspari_sq(dist_sq):
    inverse = lax.rsqrt(jnp.maximum(dist_sq, 1e-12))
    z = dist_sq * inverse * (2.0 / RAD)
    near = (((-0.25 * z + 0.5) * z + 0.625) * z - 5.0 / 3.0) * (z * z) + 1.0
    far = (
        ((((z * (1.0 / 12.0) - 0.5) * z + 0.625) * z + 5.0 / 3.0) * z - 5.0) * z
        + 4.0
        - inverse * (RAD / 3.0)
    )
    return jnp.where(z <= 1.0, near, jnp.where(z < 2.0, far, 0.0))


def split(value):
    high = value.astype(jnp.bfloat16)
    low = (value - high.astype(jnp.float32)).astype(jnp.bfloat16)
    return high, low


def rounded(value):
    high = lax.reduce_precision(value, 8, 7)
    return high.astype(jnp.bfloat16), (value - high).astype(jnp.bfloat16)


def pick_kernel(rows_ref, cols_ref, members_ref, out_ref):
    sectors, slots = rows_ref.shape
    planes = out_ref.shape[1]
    clon = out_ref.shape[2]
    clat = members_ref.shape[0] // (planes * sectors)
    lane = lax.broadcasted_iota(jnp.int32, (planes, clon), 1)
    for sector in range(sectors):

        def step(slot, acc):
            row = rows_ref[sector, slot]
            col = cols_ref[sector, slot]
            slab = members_ref[pl.ds(sector * planes * clat + row, planes, stride=clat), :]
            moved = pltpu.roll(slab, lax.rem(slot - col + clon, clon), 1)
            return jnp.where(lane == slot, moved, acc)

        out_ref[sector] = lax.fori_loop(0, slots, step, jnp.zeros((planes, clon), jnp.float32), unroll=8)


def update_kernel(first, lo, hi, lat_ref, dx2_ref, prior_ref, coef_ref, state_ref, out_ref, *, full):
    rows = state_ref.shape[0] // (2 * full)

    def one_row(y, carry):
        cell_lat = (first + y).astype(jnp.float32)
        state = jnp.concatenate(
            [state_ref[pl.ds(l * rows + y, full, stride=2 * rows), :] for l in range(2)], axis=1
        )
        for batch in range(NBATCH):
            dy = lat_ref[batch, lo:hi, :] - cell_lat
            taper = gaspari_sq(dx2_ref[batch, lo:hi, :] + dy * dy)
            pert = state - jnp.mean(state, axis=0, keepdims=True)
            high, low = split(pert)
            stacked = jnp.concatenate([high, high, low], axis=0)
            cov = jnp.dot(prior_ref[batch, lo:hi, :], stacked, preferred_element_type=jnp.float32)
            ghigh, glow = split(cov * jnp.concatenate([taper, taper], axis=1))
            both = jnp.dot(coef_ref[batch, :, lo:hi], ghigh, preferred_element_type=jnp.float32)
            rest = jnp.dot(coef_ref[batch, :full, lo:hi], glow, preferred_element_type=jnp.float32)
            state = state + (both[:full] + (both[full:] + rest))
        clon = out_ref.shape[1]
        for l in range(2):
            out_ref[pl.ds(l * rows + y, full, stride=2 * rows), :] = state[:, l * clon : (l + 1) * clon]
        return carry

    lax.fori_loop(0, rows, one_row, 0)


def body(members, obs_row, obs_col, obs_value, obs_error, obs_weight, obs_count):
    parts = lax.axis_size("lon")
    group, levels, clat, nlon = members.shape
    full = group * parts
    clon = nlon // parts
    slots = obs_row.shape[-1]
    lat_first = lax.axis_index("lat") * clat
    lon_first = lax.axis_index("lon") * clon
    half = 0.5 * nlon

    places = jnp.concatenate([obs_row.reshape(1, -1), obs_col.reshape(1, -1)], axis=1)
    places = lax.all_gather(places, "lon", axis=0, tiled=True)
    sent = members.reshape(group, levels, clat, parts, clon).transpose(3, 0, 1, 2, 4)
    planes = group * levels
    picked = pl.pallas_call(
        pick_kernel,
        grid_spec=pltpu.PrefetchScalarGridSpec(
            num_scalar_prefetch=2,
            grid=(1,),
            in_specs=[pl.BlockSpec((parts * planes * clat, clon), lambda i, *_: (0, 0))],
            out_specs=pl.BlockSpec((parts, planes, clon), lambda i, *_: (0, 0, 0)),
        ),
        out_shape=jax.ShapeDtypeStruct((parts, planes, clon), jnp.float32),
        compiler_params=pltpu.CompilerParams(vmem_limit_bytes=48 << 20),
    )(places[:, : NBATCH * slots], places[:, NBATCH * slots :], sent.reshape(-1, clon))
    picked = lax.all_to_all(picked, "lon", split_axis=0, concat_axis=0, tiled=True)
    picked = picked.reshape(full, levels, clon)

    def packed_for(batch, points):
        prior = jnp.sum(points * obs_weight[batch, 0, 0][None], axis=1)
        valid = (jnp.arange(slots) < obs_count[batch, 0, 0]).astype(jnp.float32)
        prior_mean = jnp.mean(prior, axis=0)
        prior_pert = prior - prior_mean
        spread = jnp.sum(prior_pert * prior_pert, axis=0) / (full - 1.0)
        err = obs_error[batch, 0, 0]
        denom = spread + err
        mean_coef = valid * (obs_value[batch, 0, 0] - prior_mean) / denom
        pert_coef = valid / (denom * (1.0 + jnp.sqrt(err / denom)))
        glat = (lat_first + obs_row[batch, 0, 0]).astype(jnp.float32)
        glon = (lon_first + obs_col[batch, 0, 0]).astype(jnp.float32)
        extra = jnp.stack([mean_coef, pert_coef, glat, glon], axis=0)
        packed = jnp.concatenate([prior_pert, extra], axis=0)
        wide = extended(packed[:, None, None, :], (("lat", 1), ("lon", 2)), 1)
        received = wide.reshape(packed.shape[0], -1)
        prior_pert = received[:full]
        coef = received[full][None] - received[full + 1][None] * prior_pert
        return prior_pert * (1.0 / (full - 1.0)), coef, received[full + 2], received[full + 3]

    def lon_gap(first, second):
        return jnp.mod(first - second + half, 1.0 * nlon) - half

    one = packed_for(0, picked[:, :, :slots])
    points = picked[:, :, slots : 2 * slots]
    pert = points - jnp.mean(points, axis=0)
    dy = (lat_first + obs_row[1, 0, 0]).astype(jnp.float32)[None] - one[2][:, None]
    dx = lon_gap((lon_first + obs_col[1, 0, 0]).astype(jnp.float32)[None], one[3][:, None])
    taper = gaspari_sq(dx * dx + dy * dy)
    cov = jnp.einsum("ko,klp->olp", one[0], pert, precision=HIGHEST) * taper[:, None]
    points = points + jnp.einsum("ko,olp->klp", one[1], cov, precision=HIGHEST)
    two = packed_for(1, points)

    cell_lon = (lon_first + jnp.arange(clon)).astype(jnp.float32)
    lats, gaps, priors, coefs = [], [], [], []
    for prior_pert, coef, lat, lon in (one, two):
        lats.append(jnp.broadcast_to(lat[:, None], (lat.shape[0], clon)))
        dx = lon_gap(cell_lon[None], lon[:, None])
        gaps.append(dx * dx)
        high, low = rounded(prior_pert.T)
        priors.append(jnp.concatenate([high, low, high], axis=1))
        coefs.append(jnp.concatenate(rounded(coef), axis=0))
    lats, gaps, priors, coefs = (jnp.stack(v) for v in (lats, gaps, priors, coefs))

    rows = clat // CHUNKS
    third = lats.shape[1] // 3
    shifted = lats - lat_first.astype(jnp.float32)
    results = []
    for chunk in range(CHUNKS):
        first = chunk * rows
        low = 0 if first + 1 < RAD else third
        high = 3 * third if clat - (first + rows - 1) < RAD else 2 * third
        block = lax.all_to_all(
            sent[:, :, :, first : first + rows], "lon", split_axis=0, concat_axis=0, tiled=True
        )
        obs = 2 * NBATCH * (high - low) * full * levels * rows * clon
        done = pl.pallas_call(
            functools.partial(update_kernel, first, low, high, full=full),
            out_shape=jax.ShapeDtypeStruct((full * levels * rows, clon), jnp.float32),
            in_specs=[pl.BlockSpec(memory_space=pltpu.VMEM)] * 5,
            out_specs=pl.BlockSpec(memory_space=pltpu.VMEM),
            cost_estimate=pl.CostEstimate(flops=8 * obs, bytes_accessed=1 << 23, transcendentals=0),
            compiler_params=pltpu.CompilerParams(vmem_limit_bytes=32 << 20),
        )(shifted, gaps, priors, coefs, block.reshape(-1, clon))
        back = lax.all_to_all(
            done.reshape(parts, group, levels, rows, clon), "lon", split_axis=0, concat_axis=0, tiled=True
        )
        results.append(back.transpose(1, 2, 3, 0, 4).reshape(group, levels, rows, nlon))
    return jnp.concatenate(results, axis=2)


def solution(mesh):
    placed = (
        P("lon", None, "lat", None),
        P(None, "lat", "lon", None),
        P(None, "lat", "lon", None),
        P(None, "lat", "lon", None),
        P(None, "lat", "lon", None),
        P(None, "lat", "lon", None, None),
        P(None, "lat", "lon"),
    )
    return jax.shard_map(
        body, mesh=mesh, in_specs=placed, out_specs=P("lon", None, "lat", None), check_vma=False
    )
```

time: 852 us -> 356 us (0.42); the launches traced: 839 us -> 355 us
  local copies, waits for them, and re-layouts: 274 us -> 30.9 us
  other arithmetic: 138 us -> 12.2 us
  matrix products: 123 us -> 0.93 us
  Pallas kernels: 0 us -> 118 us
  blocking collectives: 119 us -> 13.4 us
  loops' own time: 49.7 us -> 0 us
  starting transfers between devices: 19.8 us -> 47.8 us
  waiting for transfers between devices: 115 us -> 131 us
    dot_general x18 -> x0, matrix products: 123 us -> none  [the longest x8 62.8 us: one_block(): jnp.einsum('kpc,km->pcm', block, prior_pert, precision=highest)]
    all_to_all x1 -> x0, blocking collectives: 119 us -> none  [body(): return lax.all_to_all(state, 'lon', split_axis=0, concat_axis=3, tiled=True)]
    pallas_call x0 -> x5, Pallas kernels: none -> 118 us  [the longest x4 96.8 us: body(): pl.pallas_call(functools.partial(update_kernel, first, low, high, full=fu...]
    dynamic_update_slice x8 -> x0, local copies, waits for them, and re-layouts: 102 us -> none  [body(): increments = lax.map(one_block, (blocks, jnp.arange(block_count)))]
    mul x8 -> x2, other arithmetic: 77.2 us -> 0.47 us  [the longest x1 0.44 us: body(): gaps.append(dx * dx)]
    another operation x2 -> x0, loops' own time: 49.7 us -> none  [body(): increments = lax.map(one_block, (blocks, jnp.arange(block_count)))]
    all_to_all x6 -> x0, local copies, waits for them, and re-layouts: 42.2 us -> none  [the longest x5 39.1 us: body(): lax.all_to_all(members, 'lon', split_axis=3, concat_axis=0, tiled=True)]
    dynamic_slice x16 -> x0, local copies, waits for them, and re-layouts: 36.2 us -> none  [body(): increments = lax.map(one_block, (blocks, jnp.arange(block_count)))]
  transfers between devices with their start and end apart: 9 -> 17, of which waited for: 1 -> 14; matrix products, arithmetic and copies ran while one was open for 6% -> 7% of each run, Pallas kernels for 0% -> 27%
where the time goes in v1:
time: 356 us; the launch traced here: 355 us
  waiting for transfers between devices  131 us (37%)
  Pallas kernels  118 us (33%)
  starting transfers between devices  47.8 us (13%)
  local copies, waits for them, and re-layouts  30.9 us (9%)
  blocking collectives  13.4 us (4%)
  other arithmetic  12.2 us (3%)
    pallas_call x4, Pallas kernels, body(): pl.pallas_call(functools.partial(update_kernel, first, low, high, full=fu...  96.8 us
    all_to_all x4, waiting for transfers between devices, body(): lax.all_to_all(sent[:, :, :, first:first + rows], 'lon', split_axis=0, co...  56.6 us
    all_to_all x4, waiting for transfers between devices, body(): lax.all_to_all(done.reshape(parts, group, levels, rows, clon), 'lon', spl...  48.5 us
    pallas_call x1, Pallas kernels, body(): pl.pallas_call(pick_kernel, grid_spec=pltpu.PrefetchScalarGridSpec(num_sc...  21.3 us
    all_to_all x4, starting transfers between devices, body(): lax.all_to_all(done.reshape(parts, group, levels, rows, clon), 'lon', spl...  18.2 us
    all_to_all x4, starting transfers between devices, body(): lax.all_to_all(sent[:, :, :, first:first + rows], 'lon', split_axis=0, co...  16.3 us
    ppermute x4, waiting for transfers between devices, extended(): lax.ppermute(lax.slice_in_dim(block, 0, width, axis=dim), axis, backward)  14.8 us
    all_gather x1, blocking collectives, body(): places = lax.all_gather(places, 'lon', axis=0, tiled=True)  13.4 us
  transfers between devices with their start and end apart: 17, of which 14 were waited for; matrix products, arithmetic and copies ran while one was open for 7% of the time, Pallas kernels for 27%

profile of v1, /device:TPU:0, one launch (start us, length us, event | category | flops | bytes accessed | tf_op | source)
XLA Modules:
  0.0 354.7 jit_solution(8081748759005660263)
XLA Ops:
  0.0 0.5 broadcast.559
  0.5 1.3 reduce.25
  1.9 1.3 reduce.24
  3.4 13.4 %all-gather = s32[8,1,256]{2,1,0:T(1,128)S(1)} all-gather(s32[1,1,256]{2,1,0:T(1,128)S(1)} %add_bitcast_fusion), channel_id=1, replica_groups=mesh['lat'=4,'lon'=8] {'lon'}, dimensions={0}, use_global_device_ids=true | all-gather | bytes 9216 | tf_op jit(solution)/shard_map/all_gather | solution.py:108
  16.8 5.6 %fusion.37 = (f32[8,10,2,64,128]{4,3,2,1,0:T(8,128)}, f32[10,2,64,8,128]{4,2,1,0,3:T(8,128)S(1)}) fusion(f32[10,2,64,1024]{3,2,1,0:T(8,128)} %param.7), kind=kLoop, calls=%fused_computation.119 | loop fusion | bytes 15728640 | tf_op jit(solution)/shard_map/transpose | solution.py:109
  22.4 21.3 %shard_map.73 = f32[8,20,128]{2,1,0:T(8,128)} custom-call(s32[8,128]{1,0:T(8,128)S(1)} %get-tuple-element.38.rows_ref, s32[8,128]{1,0:T(8,128)S(1)} %get-tuple-element.37.cols_ref, f32[10240,128]{1,0:T(8,128)S(1)} %bitcast.138), custom_call_target="tpu_custom_call" | custom-call | tf_op jit(solution)/shard_map/pallas_call | solution.py:111
  43.6 3.4 all-to-all-start
  47.0 5.2 %fusion.38 = (f32[8,10,2,16,128]{4,3,2,1,0:T(8,128)}, f32[8,10,2,16,128]{4,3,2,1,0:T(8,128)}, f32[8,10,2,16,128]{4,3,2,1,0:T(8,128)}, f32[8,10,2,16,128]{4,3,2,1,0:T(8,128)}) fusion(f32[8,10,2,64,128]{4,3,2,1,0:T(8,128)} %get-tuple-element.26), kind=kLoop, calls=%fused_computation.120 | loop fusion | bytes 10485760 | tf_op jit(solution)/shard_map/slice | solution.py:178
  52.2 1.1 all-to-all-done
  53.3 3.9 %all-to-all-start.1 = ((f32[8,10,2,16,128]{4,3,2,1,0:T(8,128)}), f32[8,10,2,16,128]{4,3,2,1,0:T(8,128)S(1)}, u32[]{:S(2)}, u32[]{:S(2)}) async-start(f32[8,10,2,16,128]{4,3,2,1,0:T(8,128)} %get-tuple-element.22), calls=%async_computation.1 | async-start | bytes 2621440 | tf_op jit(solution)/shard_map/all_to_all | solution.py:177
  57.2 32.2 %all-to-all-done.1 = f32[8,10,2,16,128]{4,3,2,1,0:T(8,128)S(1)} async-done(((f32[8,10,2,16,128]{4,3,2,1,0:T(8,128)}), f32[8,10,2,16,128]{4,3,2,1,0:T(8,128)S(1)}, u32[]{:S(2)}, u32[]{:S(2)}) %all-to-all-start.1) | async-done | bytes 1310752 | tf_op jit(solution)/shard_map/all_to_all | solution.py:177
  89.5 3.7 %all-to-all-start.5 = ((f32[8,10,2,16,128]{4,3,2,1,0:T(8,128)}), f32[8,10,2,16,128]{4,3,2,1,0:T(8,128)S(1)}, u32[]{:S(2)}, u32[]{:S(2)}) async-start(f32[8,10,2,16,128]{4,3,2,1,0:T(8,128)} %get-tuple-element.23), calls=%async_computation.5 | async-start | bytes 2621440 | tf_op jit(solution)/shard_map/all_to_all | solution.py:177
  93.4 0.6 fusion.40
  94.3 0.6 fusion.33
  95.0 2.5 collective-permute-start.1
  97.6 1.5 collective-permute-done.1
  99.1 3.2 collective-permute-done
  102.3 2.4 collective-permute-start.3
  104.8 12.6 %collective-permute-done.3 = f32[84,3,1,64]{0,3,2,1:T(8,128)S(1)} collective-permute-done((f32[84,3,1,64]{0,3,2,1:T(8,128)S(1)}, f32[84,3,1,64]{0,3,2,1:T(8,128)S(1)}, u32[]{:S(2)}, u32[]{:S(2)}) %collective-permute-start.3) | collective-permute-done | bytes 64544 | tf_op jit(solution)/shard_map/ppermute | solution.py:24
  117.4 3.5 collective-permute-done.2
  120.9 0.7 slice_reduce_fusion.6
  121.8 4.5 %all-to-all-done.5 = f32[8,10,2,16,128]{4,3,2,1,0:T(8,128)S(1)} async-done(((f32[8,10,2,16,128]{4,3,2,1,0:T(8,128)}), f32[8,10,2,16,128]{4,3,2,1,0:T(8,128)S(1)}, u32[]{:S(2)}, u32[]{:S(2)}) %all-to-all-start.5) | async-done | bytes 1310752 | tf_op jit(solution)/shard_map/all_to_all | solution.py:177
  126.4 4.3 %all-to-all-start.3 = ((f32[8,10,2,16,128]{4,3,2,1,0:T(8,128)}), f32[8,10,2,16,128]{4,3,2,1,0:T(8,128)}, u32[]{:S(2)}, u32[]{:S(2)}) async-start(f32[8,10,2,16,128]{4,3,2,1,0:T(8,128)} %get-tuple-element.24), calls=%async_computation.3 | async-start | bytes 2621440 | tf_op jit(solution)/shard_map/all_to_all | solution.py:177
  131.3 0.5 fusion.12
  131.8 0.4 fusion.24
  132.7 0.7 fusion.35
  133.6 2.5 collective-permute-start.5
  136.2 0.7 reduce-precision_convert_fusion.3
  137.1 0.6 collective-permute-done.5
  137.8 3.2 collective-permute-done.4
  141.0 0.7 pad_maximum_fusion.7
  141.6 2.4 collective-permute-start.7
  144.1 19.8 %all-to-all-done.3 = f32[8,10,2,16,128]{4,3,2,1,0:T(8,128)} async-done(((f32[8,10,2,16,128]{4,3,2,1,0:T(8,128)}), f32[8,10,2,16,128]{4,3,2,1,0:T(8,128)}, u32[]{:S(2)}, u32[]{:S(2)}) %all-to-all-start.3) | async-done | bytes 1310752 | tf_op jit(solution)/shard_map/all_to_all | solution.py:177
  163.9 4.4 %all-to-all-start.7 = ((f32[8,10,2,16,128]{4,3,2,1,0:T(8,128)}), f32[8,10,2,16,128]{4,3,2,1,0:T(8,128)}, u32[]{:S(2)}, u32[]{:S(2)}) async-start(f32[8,10,2,16,128]{4,3,2,1,0:T(8,128)} %get-tuple-element.25), calls=%async_computation.7 | async-start | bytes 2621440 | tf_op jit(solution)/shard_map/all_to_all | solution.py:177
  168.4 1.0 pad_maximum_fusion.5
  169.4 0.7 slice_reduce_fusion.1
  170.5 0.8 copy.43
  171.3 1.0 reduce-precision_convert_fusion.2
  172.8 0.4 fusion.3
  173.6 0.5 copy-done.2
  174.1 27.1 %shard_map.75 = f32[2560,128]{1,0:T(8,128)S(1)} custom-call(f32[2,576,128]{2,1,0:T(8,128)S(1)} %maximum_subtract_fusion.lat_ref, f32[2,576,128]{2,1,0:T(8,128)S(1)} %pad_maximum_fusion.1.dx2_ref, bf16[2,576,240]{2,1,0:T(8,128)(2,1)S(1)} %pad_maximum_fusion.2.prior_ref, bf16[2,160,576]{2,1,0:T(8,128)(2,1)S(1)} %pad_maximum_fusion.3.coef_ref, ...), custom_call_target="tpu_custom_call" | custom-call | flops 6039797760 | bytes 8388608 | tf_op jit(solution)/shard_map/pallas_call | solution.py:181
  201.2 1.0 copy-done
  202.3 0.8 copy-done.5
  203.1 5.0 %all-to-all-start.4 = ((f32[8,10,2,16,128]{4,3,2,1,0:T(8,128)}), f32[8,10,2,16,128]{4,3,2,1,0:T(8,128)}, u32[]{:S(2)}, u32[]{:S(2)}) async-start(f32[8,10,2,16,128]{4,3,2,1,0:T(8,128)} %bitcast.141), calls=%async_computation.4 | async-start | bytes 2621440 | tf_op jit(solution)/shard_map/all_to_all | solution.py:189
  208.1 1.1 copy-done.3
  209.2 1.1 copy-done.6
  210.2 1.0 copy-done.9
  211.2 20.2 %shard_map.74 = f32[2560,128]{1,0:T(8,128)S(1)} custom-call(f32[2,576,128]{2,1,0:T(8,128)S(1)} %copy-done.6, f32[2,576,128]{2,1,0:T(8,128)S(1)} %copy-done.3, bf16[2,576,240]{2,1,0:T(8,128)(2,1)S(1)} %pad_maximum_fusion.2.prior_ref, bf16[2,160,576]{2,1,0:T(8,128)(2,1)S(1)} %copy-done.9, f32[2560,128]{1,0:T(8,128)S(1)} %bitcast.139), custom_call_target="tpu_custom_call" | custom-call | flops 4026531840 | bytes 8388608 | tf_op jit(solution)/shard_map/pallas_call | solution.py:181
  231.4 1.0 copy-done.1
  232.5 7.9 %all-to-all-done.4 = f32[8,10,2,16,128]{4,3,2,1,0:T(8,128)} async-done(((f32[8,10,2,16,128]{4,3,2,1,0:T(8,128)}), f32[8,10,2,16,128]{4,3,2,1,0:T(8,128)}, u32[]{:S(2)}, u32[]{:S(2)}) %all-to-all-start.4) | async-done | bytes 1310752 | tf_op jit(solution)/shard_map/all_to_all | solution.py:189
  240.4 4.6 %all-to-all-start.2 = ((f32[8,10,2,16,128]{4,3,2,1,0:T(8,128)}), f32[8,10,2,16,128]{4,3,2,1,0:T(8,128)}, u32[]{:S(2)}, u32[]{:S(2)}) async-start(f32[8,10,2,16,128]{4,3,2,1,0:T(8,128)} %bitcast.142), calls=%async_computation.2 | async-start | bytes 2621440 | tf_op jit(solution)/shard_map/all_to_all | solution.py:189
  245.0 1.0 copy-done.10
  246.0 26.9 %shard_map.76 = f32[2560,128]{1,0:T(8,128)} custom-call(f32[2,576,128]{2,1,0:T(8,128)S(1)} %copy-done.7, f32[2,576,128]{2,1,0:T(8,128)S(1)} %copy-done.4, bf16[2,576,240]{2,1,0:T(8,128)(2,1)S(1)} %pad_maximum_fusion.2.prior_ref, bf16[2,160,576]{2,1,0:T(8,128)(2,1)S(1)} %copy-done.10, f32[2560,128]{1,0:T(8,128)S(1)} %bitcast.140), custom_call_target="tpu_custom_call" | custom-call | flops 6039797760 | bytes 8388608 | tf_op jit(solution)/shard_map/pallas_call | solution.py:181
  272.9 4.3 %all-to-all-done.2 = f32[8,10,2,16,128]{4,3,2,1,0:T(8,128)} async-done(((f32[8,10,2,16,128]{4,3,2,1,0:T(8,128)}), f32[8,10,2,16,128]{4,3,2,1,0:T(8,128)}, u32[]{:S(2)}, u32[]{:S(2)}) %all-to-all-start.2) | async-done | bytes 1310752 | tf_op jit(solution)/shard_map/all_to_all | solution.py:189
  277.2 4.4 %all-to-all-start.6 = ((f32[8,10,2,16,128]{4,3,2,1,0:T(8,128)}), f32[8,10,2,16,128]{4,3,2,1,0:T(8,128)}, u32[]{:S(2)}, u32[]{:S(2)}) async-start(f32[8,10,2,16,128]{4,3,2,1,0:T(8,128)} %bitcast.42), calls=%async_computation.6 | async-start | bytes 2621440 | tf_op jit(solution)/shard_map/all_to_all | solution.py:189
  281.6 22.6 %shard_map.77 = f32[2560,128]{1,0:T(8,128)} custom-call(f32[2,576,128]{2,1,0:T(8,128)S(1)} %copy-done.7, f32[2,576,128]{2,1,0:T(8,128)S(1)} %copy-done.4, bf16[2,576,240]{2,1,0:T(8,128)(2,1)S(1)} %pad_maximum_fusion.2.prior_ref, bf16[2,160,576]{2,1,0:T(8,128)(2,1)S(1)} %copy-done.11, f32[2560,128]{1,0:T(8,128)} %bitcast.44.state_ref), custom_call_target="tpu_custom_call" | custom-call | flops 4026531840 | bytes 8388608 | tf_op jit(solution)/shard_map/pallas_call | solution.py:181
  304.3 9.6 %all-to-all-done.6 = f32[8,10,2,16,128]{4,3,2,1,0:T(8,128)} async-done(((f32[8,10,2,16,128]{4,3,2,1,0:T(8,128)}), f32[8,10,2,16,128]{4,3,2,1,0:T(8,128)}, u32[]{:S(2)}, u32[]{:S(2)}) %all-to-all-start.6) | async-done | bytes 1310752 | tf_op jit(solution)/shard_map/all_to_all | solution.py:189
  313.8 4.3 %all-to-all-start.8 = ((f32[8,10,2,16,128]{4,3,2,1,0:T(8,128)}), f32[8,10,2,16,128]{4,3,2,1,0:T(8,128)}, u32[]{:S(2)}, u32[]{:S(2)}) async-start(f32[8,10,2,16,128]{4,3,2,1,0:T(8,128)} %bitcast.45), calls=%async_computation.8 | async-start | bytes 2621440 | tf_op jit(solution)/shard_map/all_to_all | solution.py:189
  318.1 1.5 copy_bitcast_fusion.3
  319.6 1.5 copy_bitcast_fusion.4
  321.1 2.6 copy_bitcast_fusion.2
  323.6 26.7 %all-to-all-done.8 = f32[8,10,2,16,128]{4,3,2,1,0:T(8,128)} async-done(((f32[8,10,2,16,128]{4,3,2,1,0:T(8,128)}), f32[8,10,2,16,128]{4,3,2,1,0:T(8,128)}, u32[]{:S(2)}, u32[]{:S(2)}) %all-to-all-start.8) | async-done | bytes 1310752 | tf_op jit(solution)/shard_map/all_to_all | solution.py:189
  350.3 1.6 copy_bitcast_fusion.1
  352.0 2.6 pad_maximum_fusion
  (99 shorter events, 4.1 us)
Async XLA Ops:
  43.6 9.6 %all-to-all-start = ((f32[8,20,128]{2,1,0:T(8,128)}), f32[8,20,128]{2,1,0:T(8,128)S(1)}, u32[]{:S(2)}, u32[]{:S(2)}) async-start(f32[8,20,128]{2,1,0:T(8,128)} %shard_map.73), calls=%async_computation | async-start | bytes 196608 | tf_op jit(solution)/shard_map/all_to_all | solution.py:122
  53.3 36.1 %all-to-all-start.1 = ((f32[8,10,2,16,128]{4,3,2,1,0:T(8,128)}), f32[8,10,2,16,128]{4,3,2,1,0:T(8,128)S(1)}, u32[]{:S(2)}, u32[]{:S(2)}) async-start(f32[8,10,2,16,128]{4,3,2,1,0:T(8,128)} %get-tuple-element.22), calls=%async_computation.1 | async-start | bytes 2621440 | tf_op jit(solution)/shard_map/all_to_all | solution.py:177
  89.4 3.8 %copy-start.19 = (s32[2,1,1,64]{3,2,1,0:T(1,128)S(1)}, s32[2,1,1,64]{3,2,1,0:T(1,128)}, u32[]{:S(2)}) copy-start(s32[2,1,1,64]{3,2,1,0:T(1,128)} %param.9) | copy-start | bytes 1540
  89.4 3.8 %copy-start.20 = (s32[2,1,1,64]{3,2,1,0:T(1,128)S(1)}, s32[2,1,1,64]{3,2,1,0:T(1,128)}, u32[]{:S(2)}) copy-start(s32[2,1,1,64]{3,2,1,0:T(1,128)} %param.8) | copy-start | bytes 1540
  89.4 4.0 %copy-start.22 = (s32[2,1,1]{0,2,1:T(1,128)S(1)}, s32[2,1,1]{0,2,1:T(1,128)}, u32[]{:S(2)}) copy-start(s32[2,1,1]{0,2,1:T(1,128)} %param.13) | copy-start | bytes 28
  89.4 4.6 %copy-start.21 = (f32[2,1,1,2,64]{4,3,2,1,0:T(2,128)S(1)}, f32[2,1,1,2,64]{4,3,2,1,0:T(2,128)}, u32[]{:S(2)}) copy-start(f32[2,1,1,2,64]{4,3,2,1,0:T(2,128)} %param.12) | copy-start | bytes 3076
  89.4 4.9 %copy-start.23 = (f32[2,1,1,64]{3,2,1,0:T(1,128)S(1)}, f32[2,1,1,64]{3,2,1,0:T(1,128)}, u32[]{:S(2)}) copy-start(f32[2,1,1,64]{3,2,1,0:T(1,128)} %param.11) | copy-start | bytes 1540
  89.4 4.9 %copy-start.24 = (f32[2,1,1,64]{3,2,1,0:T(1,128)S(1)}, f32[2,1,1,64]{3,2,1,0:T(1,128)}, u32[]{:S(2)}) copy-start(f32[2,1,1,64]{3,2,1,0:T(1,128)} %param.10) | copy-start | bytes 1540
  89.5 36.9 %all-to-all-start.5 = ((f32[8,10,2,16,128]{4,3,2,1,0:T(8,128)}), f32[8,10,2,16,128]{4,3,2,1,0:T(8,128)S(1)}, u32[]{:S(2)}, u32[]{:S(2)}) async-start(f32[8,10,2,16,128]{4,3,2,1,0:T(8,128)} %get-tuple-element.23), calls=%async_computation.5 | async-start | bytes 2621440 | tf_op jit(solution)/shard_map/all_to_all | solution.py:177
  95.0 4.1 %collective-permute-start.1 = (f32[84,1,1,64]{0,3,2,1:T(8,128)S(1)}, f32[84,1,1,64]{0,3,2,1:T(8,128)S(1)}, u32[]{:S(2)}, u32[]{:S(2)}) collective-permute-start(f32[84,1,1,64]{0,3,2,1:T(8,128)S(1)} %bitcast.150), channel_id=1, source_target_pairs={{8,0},{16,8},{24,16},{0,24},{9,1},{17,9},{25,17},{1,25},{10,2},{18... | collective-permute-start | bytes 64520 | tf_op jit(solution)/shard_map/ppermute | solution.py:24
  97.5 4.8 %collective-permute-start = (f32[84,1,1,64]{0,3,2,1:T(8,128)S(1)}, f32[84,1,1,64]{0,3,2,1:T(8,128)S(1)}, u32[]{:S(2)}, u32[]{:S(2)}) collective-permute-start(f32[84,1,1,64]{0,3,2,1:T(8,128)S(1)} %bitcast.151), channel_id=1, source_target_pairs={{0,8},{8,16},{16,24},{24,0},{1,9},{9,17},{17,25},{25,1},{2,10},{10... | collective-permute-start | bytes 64520 | tf_op jit(solution)/shard_map/ppermute | solution.py:21
  102.3 15.1 %collective-permute-start.3 = (f32[84,3,1,64]{0,3,2,1:T(8,128)S(1)}, f32[84,3,1,64]{0,3,2,1:T(8,128)S(1)}, u32[]{:S(2)}, u32[]{:S(2)}) collective-permute-start(f32[84,3,1,64]{0,3,2,1:T(8,128)S(1)} %pad_maximum_fusion.6), channel_id=1, source_target_pairs={{1,0},{2,1},{3,2},{4,3},{5,4},{6,5},{7,6},{0,7},{9,8},{10,9},{11,1... | collective-permute-start | bytes 193544 | tf_op jit(solution)/shard_map/ppermute | solution.py:24
  104.7 16.2 %collective-permute-start.2 = (f32[84,3,1,64]{0,3,2,1:T(8,128)S(1)}, f32[84,3,1,64]{0,3,2,1:T(8,128)S(1)}, u32[]{:S(2)}, u32[]{:S(2)}) collective-permute-start(f32[84,3,1,64]{0,3,2,1:T(8,128)S(1)} %pad_maximum_fusion.6), channel_id=1, source_target_pairs={{0,1},{1,2},{2,3},{3,4},{4,5},{5,6},{6,7},{7,0},{8,9},{9,10},{10,1... | collective-permute-start | bytes 193544 | tf_op jit(solution)/shard_map/ppermute | solution.py:21
  126.4 37.5 %all-to-all-start.3 = ((f32[8,10,2,16,128]{4,3,2,1,0:T(8,128)}), f32[8,10,2,16,128]{4,3,2,1,0:T(8,128)}, u32[]{:S(2)}, u32[]{:S(2)}) async-start(f32[8,10,2,16,128]{4,3,2,1,0:T(8,128)} %get-tuple-element.24), calls=%async_computation.3 | async-start | bytes 2621440 | tf_op jit(solution)/shard_map/all_to_all | solution.py:177
  133.6 4.1 %collective-permute-start.5 = (f32[84,1,1,64]{0,3,2,1:T(8,128)S(1)}, f32[84,1,1,64]{0,3,2,1:T(8,128)S(1)}, u32[]{:S(2)}, u32[]{:S(2)}) collective-permute-start(f32[84,1,1,64]{0,3,2,1:T(8,128)S(1)} %bitcast.154), channel_id=1, source_target_pairs={{8,0},{16,8},{24,16},{0,24},{9,1},{17,9},{25,17},{1,25},{10,2},{18... | collective-permute-start | bytes 64520 | tf_op jit(solution)/shard_map/ppermute | solution.py:24
  136.2 4.8 %collective-permute-start.4 = (f32[84,1,1,64]{0,3,2,1:T(8,128)S(1)}, f32[84,1,1,64]{0,3,2,1:T(8,128)S(1)}, u32[]{:S(2)}, u32[]{:S(2)}) collective-permute-start(f32[84,1,1,64]{0,3,2,1:T(8,128)S(1)} %bitcast.155), channel_id=1, source_target_pairs={{0,8},{8,16},{16,24},{24,0},{1,9},{9,17},{17,25},{25,1},{2,10},{10... | collective-permute-start | bytes 64520 | tf_op jit(solution)/shard_map/ppermute | solution.py:21
  137.8 3.2 copy-start.15
  141.0 0.7 copy-start.17
  141.6 26.8 %collective-permute-start.7 = (f32[84,3,1,64]{0,3,2,1:T(8,128)}, f32[84,3,1,64]{0,3,2,1:T(8,128)}, u32[]{:S(2)}, u32[]{:S(2)}) collective-permute-start(f32[84,3,1,64]{0,3,2,1:T(8,128)} %pad_maximum_fusion.7), channel_id=1, source_target_pairs={{1,0},{2,1},{3,2},{4,3},{5,4},{6,5},{7,6},{0,7},{9,8},{10,9},{11,1... | collective-permute-start | bytes 193544 | tf_op jit(solution)/shard_map/ppermute | solution.py:24
  144.1 24.3 %collective-permute-start.6 = (f32[84,3,1,64]{0,3,2,1:T(8,128)}, f32[84,3,1,64]{0,3,2,1:T(8,128)}, u32[]{:S(2)}, u32[]{:S(2)}) collective-permute-start(f32[84,3,1,64]{0,3,2,1:T(8,128)} %pad_maximum_fusion.7), channel_id=1, source_target_pairs={{0,1},{1,2},{2,3},{3,4},{4,5},{5,6},{6,7},{7,0},{8,9},{9,10},{10,1... | collective-permute-start | bytes 193544 | tf_op jit(solution)/shard_map/ppermute | solution.py:21
  163.9 4.4 %copy-start.13 = (bf16[80,576]{1,0:T(8,128)(2,1)S(1)}, bf16[80,576]{1,0:T(8,128)(2,1)}, u32[]{:S(2)}) copy-start(bf16[80,576]{1,0:T(8,128)(2,1)} %get-tuple-element.32) | copy-start | bytes 276484
  163.9 4.4 %copy-start.14 = (bf16[80,576]{1,0:T(8,128)(2,1)S(1)}, bf16[80,576]{1,0:T(8,128)(2,1)}, u32[]{:S(2)}) copy-start(bf16[80,576]{1,0:T(8,128)(2,1)} %get-tuple-element.33) | copy-start | bytes 276484
  163.9 4.5 %copy-start.16 = (f32[84,1,1,64]{0,3,2,1:T(8,128)S(1)}, f32[84,1,1,64]{0,3,2,1:T(8,128)}, u32[]{:S(2)}) copy-start(f32[84,1,1,64]{0,3,2,1:T(8,128)} %copy-done.15) | copy-start | bytes 64516
  163.9 4.5 %copy-start.18 = (f32[84,1,1,64]{0,3,2,1:T(8,128)S(1)}, f32[84,1,1,64]{0,3,2,1:T(8,128)}, u32[]{:S(2)}) copy-start(f32[84,1,1,64]{0,3,2,1:T(8,128)} %copy-done.17) | copy-start | bytes 64516
  163.9 39.2 %all-to-all-start.7 = ((f32[8,10,2,16,128]{4,3,2,1,0:T(8,128)}), f32[8,10,2,16,128]{4,3,2,1,0:T(8,128)}, u32[]{:S(2)}, u32[]{:S(2)}) async-start(f32[8,10,2,16,128]{4,3,2,1,0:T(8,128)} %get-tuple-element.25), calls=%async_computation.7 | async-start | bytes 2621440 | tf_op jit(solution)/shard_map/all_to_all | solution.py:177
  172.6 1.0 copy-start.8
  173.3 0.8 copy-start.2
  201.2 1.1 copy-start
  202.3 0.8 copy-start.5
  203.1 37.3 %all-to-all-start.4 = ((f32[8,10,2,16,128]{4,3,2,1,0:T(8,128)}), f32[8,10,2,16,128]{4,3,2,1,0:T(8,128)}, u32[]{:S(2)}, u32[]{:S(2)}) async-start(f32[8,10,2,16,128]{4,3,2,1,0:T(8,128)} %bitcast.141), calls=%async_computation.4 | async-start | bytes 2621440 | tf_op jit(solution)/shard_map/all_to_all | solution.py:189
  208.1 1.1 copy-start.3
  209.2 1.1 copy-start.6
  210.2 1.0 copy-start.9
  231.4 1.1 copy-start.1
  240.4 4.6 %copy-start.4 = (f32[2,576,128]{2,1,0:T(8,128)S(1)}, f32[2,576,128]{2,1,0:T(8,128)}, u32[]{:S(2)}) copy-start(f32[2,576,128]{2,1,0:T(8,128)} %copy-done.2) | copy-start | bytes 1769476
  240.4 4.6 %copy-start.7 = (f32[2,576,128]{2,1,0:T(8,128)S(1)}, f32[2,576,128]{2,1,0:T(8,128)}, u32[]{:S(2)}) copy-start(f32[2,576,128]{2,1,0:T(8,128)} %copy-done.5) | copy-start | bytes 1769476
  240.4 36.8 %all-to-all-start.2 = ((f32[8,10,2,16,128]{4,3,2,1,0:T(8,128)}), f32[8,10,2,16,128]{4,3,2,1,0:T(8,128)}, u32[]{:S(2)}, u32[]{:S(2)}) async-start(f32[8,10,2,16,128]{4,3,2,1,0:T(8,128)} %bitcast.142), calls=%async_computation.2 | async-start | bytes 2621440 | tf_op jit(solution)/shard_map/all_to_all | solution.py:189
  245.0 1.0 copy-start.10
  277.2 4.4 %copy-start.11 = (bf16[2,160,576]{2,1,0:T(8,128)(2,1)S(1)}, bf16[2,160,576]{2,1,0:T(8,128)(2,1)}, u32[]{:S(2)}) copy-start(bf16[2,160,576]{2,1,0:T(8,128)(2,1)} %copy-done.8) | copy-start | bytes 1105924
  277.2 36.6 %all-to-all-start.6 = ((f32[8,10,2,16,128]{4,3,2,1,0:T(8,128)}), f32[8,10,2,16,128]{4,3,2,1,0:T(8,128)}, u32[]{:S(2)}, u32[]{:S(2)}) async-start(f32[8,10,2,16,128]{4,3,2,1,0:T(8,128)} %bitcast.42), calls=%async_computation.6 | async-start | bytes 2621440 | tf_op jit(solution)/shard_map/all_to_all | solution.py:189
  313.8 36.5 %all-to-all-start.8 = ((f32[8,10,2,16,128]{4,3,2,1,0:T(8,128)}), f32[8,10,2,16,128]{4,3,2,1,0:T(8,128)}, u32[]{:S(2)}, u32[]{:S(2)}) async-start(f32[8,10,2,16,128]{4,3,2,1,0:T(8,128)} %bitcast.45), calls=%async_computation.8 | async-start | bytes 2621440 | tf_op jit(solution)/shard_map/all_to_all | solution.py:189
  350.3 1.7 copy-start.12

commit v2 on v1

--- a/solution.py
+++ b/solution.py
@@ -9,7 +9,6 @@
 
 NBATCH = 2
 RAD = 48
-CHUNKS = 4
 HIGHEST = lax.Precision.HIGHEST
 
 
@@ -67,31 +66,35 @@
         out_ref[sector] = lax.fori_loop(0, slots, step, jnp.zeros((planes, clon), jnp.float32), unroll=8)
 
 
-def update_kernel(first, lo, hi, lat_ref, dx2_ref, prior_ref, coef_ref, state_ref, out_ref, *, full):
-    rows = state_ref.shape[0] // (2 * full)
-
-    def one_row(y, carry):
-        cell_lat = (first + y).astype(jnp.float32)
-        state = jnp.concatenate(
-            [state_ref[pl.ds(l * rows + y, full, stride=2 * rows), :] for l in range(2)], axis=1
-        )
-        for batch in range(NBATCH):
-            dy = lat_ref[batch, lo:hi, :] - cell_lat
-            taper = gaspari_sq(dx2_ref[batch, lo:hi, :] + dy * dy)
-            pert = state - jnp.mean(state, axis=0, keepdims=True)
-            high, low = split(pert)
-            stacked = jnp.concatenate([high, high, low], axis=0)
-            cov = jnp.dot(prior_ref[batch, lo:hi, :], stacked, preferred_element_type=jnp.float32)
-            ghigh, glow = split(cov * jnp.concatenate([taper, taper], axis=1))
-            both = jnp.dot(coef_ref[batch, :, lo:hi], ghigh, preferred_element_type=jnp.float32)
-            rest = jnp.dot(coef_ref[batch, :full, lo:hi], glow, preferred_element_type=jnp.float32)
-            state = state + (both[:full] + (both[full:] + rest))
-        clon = out_ref.shape[1]
-        for l in range(2):
-            out_ref[pl.ds(l * rows + y, full, stride=2 * rows), :] = state[:, l * clon : (l + 1) * clon]
-        return carry
-
-    lax.fori_loop(0, rows, one_row, 0)
+def update_kernel(pieces, lat_ref, dx2_ref, prior_ref, coef_ref, state_ref, out_ref):
+    planes, rows, clon = out_ref.shape
+    full = planes // 2
+    state_flat = state_ref.reshape(planes * rows, clon)
+    out_flat = out_ref.reshape(planes * rows, clon)
+    first = pieces[0][0]
+
+    for begin, end, lo, hi in pieces:
+
+        def one_row(y, carry):
+            cell_lat = y.astype(jnp.float32)
+            spots = [pl.ds(l * rows + y - first, full, stride=2 * rows) for l in range(2)]
+            state = jnp.concatenate([state_flat[spot, :] for spot in spots], axis=1)
+            for batch in range(NBATCH):
+                dy = lat_ref[batch, lo:hi, :] - cell_lat
+                taper = gaspari_sq(dx2_ref[batch, lo:hi, :] + dy * dy)
+                pert = state - jnp.mean(state, axis=0, keepdims=True)
+                high, low = split(pert)
+                stacked = jnp.concatenate([high, high, low], axis=0)
+                cov = jnp.dot(prior_ref[batch, lo:hi, :], stacked, preferred_element_type=jnp.float32)
+                ghigh, glow = split(cov * jnp.concatenate([taper, taper], axis=1))
+                both = jnp.dot(coef_ref[batch, :, lo:hi], ghigh, preferred_element_type=jnp.float32)
+                rest = jnp.dot(coef_ref[batch, :full, lo:hi], glow, preferred_element_type=jnp.float32)
+                state = state + (both[:full] + (both[full:] + rest))
+            for l, spot in enumerate(spots):
+                out_flat[spot, :] = state[:, l * clon : (l + 1) * clon]
+            return carry
+
+        lax.fori_loop(begin, end, one_row, 0)
 
 
 def body(members, obs_row, obs_col, obs_value, obs_error, obs_weight, obs_count):
@@ -105,8 +108,11 @@
     half = 0.5 * nlon
 
     places = jnp.concatenate([obs_row.reshape(1, -1), obs_col.reshape(1, -1)], axis=1)
+    sent = members.reshape(group, levels, clat, parts, clon).transpose(3, 0, 1, 2, 4)
+    block = lax.all_to_all(sent, "lon", split_axis=0, concat_axis=0, tiled=True)
+    block = block.reshape(full * levels, clat, clon)
+    places, sent = lax.optimization_barrier((places, sent))
     places = lax.all_gather(places, "lon", axis=0, tiled=True)
-    sent = members.reshape(group, levels, clat, parts, clon).transpose(3, 0, 1, 2, 4)
     planes = group * levels
     picked = pl.pallas_call(
         pick_kernel,
@@ -119,7 +125,8 @@
         out_shape=jax.ShapeDtypeStruct((parts, planes, clon), jnp.float32),
         compiler_params=pltpu.CompilerParams(vmem_limit_bytes=48 << 20),
     )(places[:, : NBATCH * slots], places[:, NBATCH * slots :], sent.reshape(-1, clon))
-    picked = lax.all_to_all(picked, "lon", split_axis=0, concat_axis=0, tiled=True)
+    picked = lax.all_gather(picked, "lon", axis=0, tiled=False)
+    picked = lax.dynamic_index_in_dim(picked, lax.axis_index("lon"), axis=1, keepdims=False)
     picked = picked.reshape(full, levels, clon)
 
     def packed_for(batch, points):
@@ -166,26 +173,30 @@
         coefs.append(jnp.concatenate(rounded(coef), axis=0))
     lats, gaps, priors, coefs = (jnp.stack(v) for v in (lats, gaps, priors, coefs))
 
-    rows = clat // CHUNKS
     third = lats.shape[1] // 3
     shifted = lats - lat_first.astype(jnp.float32)
+    step = clat // 4
+
+    def piece(begin, end):
+        low = 0 if begin + 1 < RAD else third
+        high = 3 * third if clat - (end - 1) < RAD else 2 * third
+        return begin, end, low, high
+
     results = []
-    for chunk in range(CHUNKS):
-        first = chunk * rows
-        low = 0 if first + 1 < RAD else third
-        high = 3 * third if clat - (first + rows - 1) < RAD else 2 * third
-        block = lax.all_to_all(
-            sent[:, :, :, first : first + rows], "lon", split_axis=0, concat_axis=0, tiled=True
-        )
-        obs = 2 * NBATCH * (high - low) * full * levels * rows * clon
+    for begin, end in ((0, step), (step, 2 * step), (2 * step, clat)):
+        rows = end - begin
+        pieces = tuple(piece(y, y + step) for y in range(begin, end, step))
+        flops = sum(16 * NBATCH * (p[3] - p[2]) * full * levels * step * clon for p in pieces)
         done = pl.pallas_call(
-            functools.partial(update_kernel, first, low, high, full=full),
-            out_shape=jax.ShapeDtypeStruct((full * levels * rows, clon), jnp.float32),
-            in_specs=[pl.BlockSpec(memory_space=pltpu.VMEM)] * 5,
-            out_specs=pl.BlockSpec(memory_space=pltpu.VMEM),
-            cost_estimate=pl.CostEstimate(flops=8 * obs, bytes_accessed=1 << 23, transcendentals=0),
-            compiler_params=pltpu.CompilerParams(vmem_limit_bytes=32 << 20),
-        )(shifted, gaps, priors, coefs, block.reshape(-1, clon))
+            functools.partial(update_kernel, pieces),
+            grid=(1,),
+            out_shape=jax.ShapeDtypeStruct((full * levels, rows, clon), jnp.float32),
+            in_specs=[pl.BlockSpec(v.shape, lambda i: (0, 0, 0)) for v in (shifted, gaps, priors, coefs)]
+            + [pl.BlockSpec((full * levels, rows, clon), lambda i, at=begin // rows: (0, at, 0))],
+            out_specs=pl.BlockSpec((full * levels, rows, clon), lambda i: (0, 0, 0)),
+            cost_estimate=pl.CostEstimate(flops=8 * flops, bytes_accessed=1 << 23, transcendentals=0),
+            compiler_params=pltpu.CompilerParams(vmem_limit_bytes=40 << 20),
+        )(shifted, gaps, priors, coefs, block)
         back = lax.all_to_all(
             done.reshape(parts, group, levels, rows, clon), "lon", split_axis=0, concat_axis=0, tiled=True
         )

time: 356 us -> 392 us (1.10)
  blocking collectives: 13.4 us -> 132 us
  waiting for transfers between devices: 131 us -> 83 us
  starting transfers between devices: 47.8 us -> 25.2 us
  local copies, waits for them, and re-layouts: 30.9 us -> 19.7 us
  Pallas kernels: 118 us -> 122 us
    all_gather x1, blocking collectives: 13.4 us -> 90.1 us  [body(): places = lax.all_gather(places, 'lon', axis=0, tiled=True)]
    all_to_all x5 -> x1, waiting for transfers between devices: 57.7 us -> 0.01 us  [body(): block = lax.all_to_all(sent, 'lon', split_axis=0, concat_axis=0, tiled=True)]
    all_gather x0 -> x1, blocking collectives: none -> 41.6 us  [body(): picked = lax.all_gather(picked, 'lon', axis=0, tiled=False)]
    all_to_all x4 -> x3, waiting for transfers between devices: 48.5 us -> 64.6 us  [body(): lax.all_to_all(done.reshape(parts, group, levels, rows, clon), 'lon', spl...]
    all_to_all x5 -> x1, starting transfers between devices: 19.7 us -> 6.46 us  [body(): block = lax.all_to_all(sent, 'lon', split_axis=0, concat_axis=0, tiled=True)]
    ppermute x4, waiting for transfers between devices: 14.8 us -> 7.66 us  [extended(): lax.ppermute(lax.slice_in_dim(block, 0, width, axis=dim), axis, backward)]
    ppermute x4, starting transfers between devices: 9.84 us -> 3.68 us  [extended(): lax.ppermute(lax.slice_in_dim(block, 0, width, axis=dim), axis, backward)]
    all_to_all x4 -> x3, starting transfers between devices: 18.2 us -> 12.8 us  [body(): lax.all_to_all(done.reshape(parts, group, levels, rows, clon), 'lon', spl...]
  transfers between devices with their start and end apart: 17 -> 12, of which waited for: 14 -> 10; matrix products, arithmetic and copies ran while one was open for 7% -> 4% of each run, Pallas kernels for 27% -> 24%
where the time goes in v2:
time: 392 us
  blocking collectives  132 us (34%)
  Pallas kernels  122 us (31%)
  waiting for transfers between devices  83 us (21%)
  starting transfers between devices  25.2 us (6%)
  local copies, waits for them, and re-layouts  19.7 us (5%)
  other arithmetic  8.33 us (2%)
    pallas_call x3, Pallas kernels, body(): pl.pallas_call(functools.partial(update_kernel, pieces), grid=(1,), out_s...  102 us
    all_gather x1, blocking collectives, body(): places = lax.all_gather(places, 'lon', axis=0, tiled=True)  90.1 us
    all_to_all x3, waiting for transfers between devices, body(): lax.all_to_all(done.reshape(parts, group, levels, rows, clon), 'lon', spl...  64.6 us
    all_gather x1, blocking collectives, body(): picked = lax.all_gather(picked, 'lon', axis=0, tiled=False)  41.6 us
    pallas_call x1, Pallas kernels, body(): pl.pallas_call(pick_kernel, grid_spec=pltpu.PrefetchScalarGridSpec(num_sc...  20.6 us
    all_to_all x3, starting transfers between devices, body(): lax.all_to_all(done.reshape(parts, group, levels, rows, clon), 'lon', spl...  12.8 us
    ppermute x4, waiting for transfers between devices, extended(): lax.ppermute(lax.slice_in_dim(block, block.shape[dim] - width, None, axis...  10.7 us
  transfers between devices with their start and end apart: 12, of which 10 were waited for; matrix products, arithmetic and copies ran while one was open for 4% of the time, Pallas kernels for 24%

profile of v2, /device:TPU:0, one launch (start us, length us, event | category | flops | bytes accessed | tf_op | source)
XLA Modules:
  0.0 391.6 jit_solution(2523406155466699044)
XLA Ops:
  0.0 5.6 %bitcast_bitcast_fusion = f32[8,10,2,64,128]{4,3,2,1,0:T(8,128)} fusion(f32[10,2,64,1024]{3,2,1,0:T(8,128)} %param.7), kind=kLoop, calls=%fused_computation | loop fusion | bytes 10485760 | tf_op jit(solution)/shard_map/transpose | solution.py:111
  5.6 6.5 %all-to-all-start = ((f32[8,10,2,64,128]{4,3,2,1,0:T(8,128)}), f32[8,10,2,64,128]{4,3,2,1,0:T(8,128)}, u32[]{:S(2)}, u32[]{:S(2)}) async-start(f32[8,10,2,64,128]{4,3,2,1,0:T(8,128)} %bitcast_bitcast_fusion), calls=%async_computation | async-start | bytes 10485760 | tf_op jit(solution)/shard_map/all_to_all | solution.py:112
  12.0 0.5 broadcast.559
  12.6 0.7 reduce.25
  13.2 0.1 reshape.572
  13.3 0.7 reduce.24
  14.0 0.1 reshape.573
  14.1 90.1 %all-gather.1 = s32[8,1,256]{2,1,0:T(1,128)S(1)} all-gather(s32[1,1,256]{2,1,0:T(1,128)S(1)} %bitcast.147), channel_id=1, replica_groups=mesh['lat'=4,'lon'=8] {'lon'}, dimensions={0}, use_global_device_ids=true | all-gather | bytes 9216 | tf_op jit(solution)/shard_map/all_gather | solution.py:115
  104.2 2.5 copy-done
  106.7 20.6 %shard_map.73 = f32[8,20,128]{2,1,0:T(8,128)S(1)} custom-call(s32[8,128]{1,0:T(8,128)S(1)} %get-tuple-element.36.rows_ref, s32[8,128]{1,0:T(8,128)S(1)} %get-tuple-element.35.cols_ref, f32[10240,128]{1,0:T(8,128)S(1)} %bitcast.127), custom_call_target="tpu_custom_call" | custom-call | tf_op jit(solution)/shard_map/pallas_call | solution.py:117
  127.3 41.6 %all-gather = f32[64,20,128]{2,0,1:T(8,128)S(1)} all-gather(f32[8,20,128]{2,0,1:T(8,128)S(1)} %copy.32), channel_id=2, replica_groups=mesh['lat'=4,'lon'=8] {'lon'}, dimensions={0}, use_global_device_ids=true | all-gather | bytes 737280 | tf_op jit(solution)/shard_map/all_gather | solution.py:128
  169.0 0.6 fusion.38
  169.7 0.2 fusion.28
  169.9 0.6 fusion.33
  170.6 0.1 copy.34
  170.7 2.5 collective-permute-start.1
  173.2 0.1 copy.49
  173.4 0.1 copy.40
  173.5 0.1 copy.41
  173.6 1.2 collective-permute-done.1
  174.8 3.2 collective-permute-done
  178.0 0.8 collective-permute-start.3
  178.8 2.4 collective-permute-done.3
  181.2 3.4 collective-permute-done.2
  184.7 0.7 slice_reduce_fusion.6
  185.7 0.2 copy.36
  185.9 0.4 select_select_fusion
  186.2 0.5 fusion.12
  186.8 0.4 fusion.24
  187.2 0.2 fusion.30
  187.4 0.2 multiply_reduce_fusion.1
  187.6 0.7 fusion.35
  188.3 0.1 copy.39
  188.3 0.1 copy.38
  188.4 0.1 concatenate.40
  188.6 0.3 collective-permute-start.5
  188.9 1.7 collective-permute-start.4
  190.7 0.2 maximum_bitcast_fusion
  191.0 1.6 collective-permute-done.5
  192.5 1.2 collective-permute-done.4
  193.8 0.5 collective-permute-start.6
  194.3 2.5 collective-permute-done.7
  196.8 2.9 collective-permute-done.6
  199.7 0.7 slice_reduce_fusion.1
  200.8 0.2 copy.42
  201.1 0.2 maximum_bitcast_fusion.1
  201.3 0.1 pad_maximum_fusion.2.prior_ref
  201.5 0.4 fusion.3
  202.0 0.1 stack_broadcast_in_dim.17
  202.1 0.1 stack_broadcast_in_dim.15
  202.3 28.2 %shard_map.75 = f32[160,16,128]{2,1,0:T(8,128)} custom-call(f32[2,576,128]{2,1,0:T(8,128)S(1)} %maximum_subtract_fusion.lat_ref, f32[2,576,128]{2,1,0:T(8,128)S(1)} %pad_maximum_fusion.1.dx2_ref, bf16[2,576,240]{2,1,0:T(8,128)(2,1)S(1)} %pad_maximum_fusion.2.prior_ref, bf16[2,160,576]{2,1,0:T(8,128)(2,1)S(1)} %pad_maximum_fusion.3.coef_ref, ...), custom_call_target="tpu_custom_call" | custom-call | flops 48318382080 | bytes 8388608 | tf_op jit(solution)/shard_map/pallas_call | solution.py:190
  230.5 3.6 all-to-all-start.2
  234.1 22.7 %shard_map.74 = f32[160,16,128]{2,1,0:T(8,128)} custom-call(f32[2,576,128]{2,1,0:T(8,128)S(1)} %maximum_subtract_fusion.lat_ref, f32[2,576,128]{2,1,0:T(8,128)S(1)} %pad_maximum_fusion.1.dx2_ref, bf16[2,576,240]{2,1,0:T(8,128)(2,1)S(1)} %pad_maximum_fusion.2.prior_ref, bf16[2,160,576]{2,1,0:T(8,128)(2,1)S(1)} %pad_maximum_fusion.3.coef_ref, ...), custom_call_target="tpu_custom_call" | custom-call | flops 32212254720 | bytes 8388608 | tf_op jit(solution)/shard_map/pallas_call | solution.py:190
  256.8 9.4 %all-to-all-done.2 = f32[8,10,2,16,128]{4,3,2,1,0:T(8,128)S(1)} async-done(((f32[8,10,2,16,128]{4,3,2,1,0:T(8,128)}), f32[8,10,2,16,128]{4,3,2,1,0:T(8,128)S(1)}, u32[]{:S(2)}, u32[]{:S(2)}) %all-to-all-start.2) | async-done | bytes 1310752 | tf_op jit(solution)/shard_map/all_to_all | solution.py:200
  266.2 4.4 %all-to-all-start.1 = ((f32[8,10,2,16,128]{4,3,2,1,0:T(8,128)}), f32[8,10,2,16,128]{4,3,2,1,0:T(8,128)}, u32[]{:S(2)}, u32[]{:S(2)}) async-start(f32[8,10,2,16,128]{4,3,2,1,0:T(8,128)} %bitcast.37), calls=%async_computation.1 | async-start | bytes 2621440 | tf_op jit(solution)/shard_map/all_to_all | solution.py:200
  270.7 50.8 %shard_map.76 = f32[160,32,128]{2,1,0:T(8,128)} custom-call(f32[2,576,128]{2,1,0:T(8,128)S(1)} %maximum_subtract_fusion.lat_ref, f32[2,576,128]{2,1,0:T(8,128)S(1)} %pad_maximum_fusion.1.dx2_ref, bf16[2,576,240]{2,1,0:T(8,128)(2,1)S(1)} %pad_maximum_fusion.2.prior_ref, bf16[2,160,576]{2,1,0:T(8,128)(2,1)S(1)} %pad_maximum_fusion.3.coef_ref, ...), custom_call_target="tpu_custom_call" | custom-call | flops 80530636800 | bytes 8388608 | tf_op jit(solution)/shard_map/pallas_call | solution.py:190
  321.5 4.8 %all-to-all-start.3 = ((f32[8,10,2,32,128]{4,3,2,1,0:T(8,128)}), f32[8,10,2,32,128]{4,3,2,1,0:T(8,128)S(1)}, u32[]{:S(2)}, u32[]{:S(2)}) async-start(f32[8,10,2,32,128]{4,3,2,1,0:T(8,128)} %bitcast.41), calls=%async_computation.3 | async-start | bytes 5242880 | tf_op jit(solution)/shard_map/all_to_all | solution.py:200
  326.3 2.5 copy_bitcast_fusion.1
  328.9 2.6 copy_bitcast_fusion.2
  331.4 55.2 %all-to-all-done.3 = f32[8,10,2,32,128]{4,3,2,1,0:T(8,128)S(1)} async-done(((f32[8,10,2,32,128]{4,3,2,1,0:T(8,128)}), f32[8,10,2,32,128]{4,3,2,1,0:T(8,128)S(1)}, u32[]{:S(2)}, u32[]{:S(2)}) %all-to-all-start.3) | async-done | bytes 2621472 | tf_op jit(solution)/shard_map/all_to_all | solution.py:200
  386.6 0.3 copy_bitcast_fusion
  387.0 1.0 copy-done.1
  387.9 0.4 copy-done.2
  388.3 3.2 pad_maximum_fusion
  (60 shorter events, 1.5 us)
Async XLA Ops:
  5.6 7.0 %copy-start.5 = (s32[2,1,1,64]{3,2,1,0:T(1,128)S(1)}, s32[2,1,1,64]{3,2,1,0:T(1,128)}, u32[]{:S(2)}) copy-start(s32[2,1,1,64]{3,2,1,0:T(1,128)} %param.8) | copy-start | bytes 1540
  5.6 7.7 %copy-start.4 = (s32[2,1,1,64]{3,2,1,0:T(1,128)S(1)}, s32[2,1,1,64]{3,2,1,0:T(1,128)}, u32[]{:S(2)}) copy-start(s32[2,1,1,64]{3,2,1,0:T(1,128)} %param.9) | copy-start | bytes 1540
  5.6 196.7 %all-to-all-start = ((f32[8,10,2,64,128]{4,3,2,1,0:T(8,128)}), f32[8,10,2,64,128]{4,3,2,1,0:T(8,128)}, u32[]{:S(2)}, u32[]{:S(2)}) async-start(f32[8,10,2,64,128]{4,3,2,1,0:T(8,128)} %bitcast_bitcast_fusion), calls=%async_computation | async-start | bytes 10485760 | tf_op jit(solution)/shard_map/all_to_all | solution.py:112
  104.2 2.5 copy-start
  106.6 62.4 %copy-start.7 = (s32[2,1,1]{0,2,1:T(1,128)S(1)}, s32[2,1,1]{0,2,1:T(1,128)}, u32[]{:S(2)}) copy-start(s32[2,1,1]{0,2,1:T(1,128)} %param.13) | copy-start | bytes 28
  106.6 63.0 %copy-start.6 = (f32[2,1,1,2,64]{4,3,2,1,0:T(2,128)S(1)}, f32[2,1,1,2,64]{4,3,2,1,0:T(2,128)}, u32[]{:S(2)}) copy-start(f32[2,1,1,2,64]{4,3,2,1,0:T(2,128)} %param.12) | copy-start | bytes 3076
  106.6 63.3 %copy-start.8 = (f32[2,1,1,64]{3,2,1,0:T(1,128)S(1)}, f32[2,1,1,64]{3,2,1,0:T(1,128)}, u32[]{:S(2)}) copy-start(f32[2,1,1,64]{3,2,1,0:T(1,128)} %param.11) | copy-start | bytes 1540
  106.6 63.3 %copy-start.9 = (f32[2,1,1,64]{3,2,1,0:T(1,128)S(1)}, f32[2,1,1,64]{3,2,1,0:T(1,128)}, u32[]{:S(2)}) copy-start(f32[2,1,1,64]{3,2,1,0:T(1,128)} %param.10) | copy-start | bytes 1540
  170.7 4.1 %collective-permute-start.1 = (f32[84,1,1,64]{0,3,2,1:T(8,128)S(1)}, f32[84,1,1,64]{0,3,2,1:T(8,128)S(1)}, u32[]{:S(2)}, u32[]{:S(2)}) collective-permute-start(f32[84,1,1,64]{0,3,2,1:T(8,128)S(1)} %bitcast.136), channel_id=1, source_target_pairs={{8,0},{16,8},{24,16},{0,24},{9,1},{17,9},{25,17},{1,25},{10,2},{18... | collective-permute-start | bytes 64520 | tf_op jit(solution)/shard_map/ppermute | solution.py:23
  173.2 4.8 %collective-permute-start = (f32[84,1,1,64]{0,3,2,1:T(8,128)S(1)}, f32[84,1,1,64]{0,3,2,1:T(8,128)S(1)}, u32[]{:S(2)}, u32[]{:S(2)}) collective-permute-start(f32[84,1,1,64]{0,3,2,1:T(8,128)S(1)} %bitcast.137), channel_id=1, source_target_pairs={{0,8},{8,16},{16,24},{24,0},{1,9},{9,17},{17,25},{25,1},{2,10},{10... | collective-permute-start | bytes 64520 | tf_op jit(solution)/shard_map/ppermute | solution.py:20
  178.0 3.2 collective-permute-start.3
  178.8 5.8 %collective-permute-start.2 = (f32[84,3,1,64]{0,3,2,1:T(8,128)S(1)}, f32[84,3,1,64]{0,3,2,1:T(8,128)S(1)}, u32[]{:S(2)}, u32[]{:S(2)}) collective-permute-start(f32[84,3,1,64]{0,3,2,1:T(8,128)S(1)} %pad_maximum_fusion.6), channel_id=1, source_target_pairs={{0,1},{1,2},{2,3},{3,4},{4,5},{5,6},{6,7},{7,0},{8,9},{9,10},{10,1... | collective-permute-start | bytes 193544 | tf_op jit(solution)/shard_map/ppermute | solution.py:20
  188.6 4.0 %collective-permute-start.5 = (f32[84,1,1,64]{0,3,2,1:T(8,128)S(1)}, f32[84,1,1,64]{0,3,2,1:T(8,128)S(1)}, u32[]{:S(2)}, u32[]{:S(2)}) collective-permute-start(f32[84,1,1,64]{0,3,2,1:T(8,128)S(1)} %bitcast.140), channel_id=1, source_target_pairs={{8,0},{16,8},{24,16},{0,24},{9,1},{17,9},{25,17},{1,25},{10,2},{18... | collective-permute-start | bytes 64520 | tf_op jit(solution)/shard_map/ppermute | solution.py:23
  188.9 4.8 %collective-permute-start.4 = (f32[84,1,1,64]{0,3,2,1:T(8,128)S(1)}, f32[84,1,1,64]{0,3,2,1:T(8,128)S(1)}, u32[]{:S(2)}, u32[]{:S(2)}) collective-permute-start(f32[84,1,1,64]{0,3,2,1:T(8,128)S(1)} %bitcast.141), channel_id=1, source_target_pairs={{0,8},{8,16},{16,24},{24,0},{1,9},{9,17},{17,25},{25,1},{2,10},{10... | collective-permute-start | bytes 64520 | tf_op jit(solution)/shard_map/ppermute | solution.py:20
  193.7 3.1 collective-permute-start.7
  193.8 5.9 %collective-permute-start.6 = (f32[84,3,1,64]{0,3,2,1:T(8,128)S(1)}, f32[84,3,1,64]{0,3,2,1:T(8,128)S(1)}, u32[]{:S(2)}, u32[]{:S(2)}) collective-permute-start(f32[84,3,1,64]{0,3,2,1:T(8,128)S(1)} %pad_maximum_fusion.7), channel_id=1, source_target_pairs={{0,1},{1,2},{2,3},{3,4},{4,5},{5,6},{6,7},{7,0},{8,9},{9,10},{10,1... | collective-permute-start | bytes 193544 | tf_op jit(solution)/shard_map/ppermute | solution.py:20
  230.5 35.7 %all-to-all-start.2 = ((f32[8,10,2,16,128]{4,3,2,1,0:T(8,128)}), f32[8,10,2,16,128]{4,3,2,1,0:T(8,128)S(1)}, u32[]{:S(2)}, u32[]{:S(2)}) async-start(f32[8,10,2,16,128]{4,3,2,1,0:T(8,128)} %bitcast.39), calls=%async_computation.2 | async-start | bytes 2621440 | tf_op jit(solution)/shard_map/all_to_all | solution.py:200
  266.2 55.3 %copy-start.3 = (f32[8,10,2,16,128]{4,3,2,1,0:T(8,128)}, f32[8,10,2,16,128]{4,3,2,1,0:T(8,128)S(1)}, u32[]{:S(2)}) copy-start(f32[8,10,2,16,128]{4,3,2,1,0:T(8,128)S(1)} %all-to-all-done.2) | copy-start | bytes 3932164
  266.2 55.3 %all-to-all-start.1 = ((f32[8,10,2,16,128]{4,3,2,1,0:T(8,128)}), f32[8,10,2,16,128]{4,3,2,1,0:T(8,128)}, u32[]{:S(2)}, u32[]{:S(2)}) async-start(f32[8,10,2,16,128]{4,3,2,1,0:T(8,128)} %bitcast.37), calls=%async_computation.1 | async-start | bytes 2621440 | tf_op jit(solution)/shard_map/all_to_all | solution.py:200
  321.5 65.1 %all-to-all-start.3 = ((f32[8,10,2,32,128]{4,3,2,1,0:T(8,128)}), f32[8,10,2,32,128]{4,3,2,1,0:T(8,128)S(1)}, u32[]{:S(2)}, u32[]{:S(2)}) async-start(f32[8,10,2,32,128]{4,3,2,1,0:T(8,128)} %bitcast.41), calls=%async_computation.3 | async-start | bytes 5242880 | tf_op jit(solution)/shard_map/all_to_all | solution.py:200
  386.6 1.3 copy-start.1
  386.6 1.7 copy-start.2

commit v3 on v2

--- a/solution.py
+++ b/solution.py
@@ -108,11 +108,11 @@
     half = 0.5 * nlon
 
     places = jnp.concatenate([obs_row.reshape(1, -1), obs_col.reshape(1, -1)], axis=1)
+    places = lax.all_gather(places, "lon", axis=0, tiled=True)
+    places, members = lax.optimization_barrier((places, members))
     sent = members.reshape(group, levels, clat, parts, clon).transpose(3, 0, 1, 2, 4)
     block = lax.all_to_all(sent, "lon", split_axis=0, concat_axis=0, tiled=True)
     block = block.reshape(full * levels, clat, clon)
-    places, sent = lax.optimization_barrier((places, sent))
-    places = lax.all_gather(places, "lon", axis=0, tiled=True)
     planes = group * levels
     picked = pl.pallas_call(
         pick_kernel,
@@ -125,8 +125,14 @@
         out_shape=jax.ShapeDtypeStruct((parts, planes, clon), jnp.float32),
         compiler_params=pltpu.CompilerParams(vmem_limit_bytes=48 << 20),
     )(places[:, : NBATCH * slots], places[:, NBATCH * slots :], sent.reshape(-1, clon))
-    picked = lax.all_gather(picked, "lon", axis=0, tiled=False)
-    picked = lax.dynamic_index_in_dim(picked, lax.axis_index("lon"), axis=1, keepdims=False)
+    me = lax.axis_index("lon")
+    rotated = lax.dynamic_slice_in_dim(jnp.concatenate([picked, picked]), me, parts)
+    arrived = [
+        lax.ppermute(rotated[shift], "lon", [(i, (i + shift) % parts) for i in range(parts)])
+        for shift in range(parts - 1, 0, -1)
+    ]
+    arrived = jnp.stack(arrived + [rotated[0]])
+    picked = lax.dynamic_slice_in_dim(jnp.concatenate([arrived, arrived]), parts - 1 - me, parts)
     picked = picked.reshape(full, levels, clon)
 
     def packed_for(batch, points):
@@ -175,18 +181,23 @@
 
     third = lats.shape[1] // 3
     shifted = lats - lat_first.astype(jnp.float32)
-    step = clat // 4
+    step = clat // 8
 
     def piece(begin, end):
         low = 0 if begin + 1 < RAD else third
         high = 3 * third if clat - (end - 1) < RAD else 2 * third
         return begin, end, low, high
 
-    results = []
-    for begin, end in ((0, step), (step, 2 * step), (2 * step, clat)):
+    results = {}
+    for begin, end in ((6 * step, clat), (0, 3 * step), (3 * step, 6 * step)):
         rows = end - begin
-        pieces = tuple(piece(y, y + step) for y in range(begin, end, step))
-        flops = sum(16 * NBATCH * (p[3] - p[2]) * full * levels * step * clon for p in pieces)
+        pieces = []
+        for y in range(begin, end, step):
+            new = piece(y, y + step)
+            if pieces and pieces[-1][2:] == new[2:]:
+                new = (pieces.pop()[0],) + new[1:]
+            pieces.append(new)
+        flops = sum(16 * NBATCH * (p[3] - p[2]) * full * levels * (p[1] - p[0]) * clon for p in pieces)
         done = pl.pallas_call(
             functools.partial(update_kernel, pieces),
             grid=(1,),
@@ -200,8 +211,8 @@
         back = lax.all_to_all(
             done.reshape(parts, group, levels, rows, clon), "lon", split_axis=0, concat_axis=0, tiled=True
         )
-        results.append(back.transpose(1, 2, 3, 0, 4).reshape(group, levels, rows, nlon))
-    return jnp.concatenate(results, axis=2)
+        results[begin] = back.transpose(1, 2, 3, 0, 4).reshape(group, levels, rows, nlon)
+    return jnp.concatenate([results[begin] for begin in sorted(results)], axis=2)
 
 
 def solution(mesh):

time: 392 us -> 359 us (0.916)
  blocking collectives: 132 us -> 13.4 us
  waiting for transfers between devices: 83 us -> 134 us
  starting transfers between devices: 25.2 us -> 62 us
  Pallas kernels: 122 us -> 118 us
    all_gather x1, blocking collectives: 90.1 us -> 13.4 us  [body(): places = lax.all_gather(places, 'lon', axis=0, tiled=True)]
    ppermute x0 -> x7, waiting for transfers between devices: none -> 59 us  [body(): lax.ppermute(rotated[shift], 'lon', [(i, (i + shift) % parts) for i in ra...]
    all_gather x1 -> x0, blocking collectives: 41.6 us -> none  [body(): picked = lax.all_gather(picked, 'lon', axis=0, tiled=False)]
    ppermute x0 -> x7, starting transfers between devices: none -> 38.6 us  [body(): lax.ppermute(rotated[shift], 'lon', [(i, (i + shift) % parts) for i in ra...]
    all_to_all x3, waiting for transfers between devices: 64.6 us -> 56.3 us  [body(): lax.all_to_all(done.reshape(parts, group, levels, rows, clon), 'lon', spl...]
    pallas_call x3, Pallas kernels: 102 us -> 96.9 us  [body(): pl.pallas_call(functools.partial(update_kernel, pieces), grid=(1,), out_s...]
  transfers between devices with their start and end apart: 12 -> 19, of which waited for: 10 -> 13; matrix products, arithmetic and copies ran while one was open for 4% -> 3% of each run, Pallas kernels for 24% -> 26%
where the time goes in v3:
time: 359 us
  waiting for transfers between devices  134 us (37%)
  Pallas kernels  118 us (33%)
  starting transfers between devices  62 us (17%)
  local copies, waits for them, and re-layouts  20.1 us (6%)
  blocking collectives  13.4 us (4%)
  other arithmetic  9.62 us (3%)
    pallas_call x3, Pallas kernels, body(): pl.pallas_call(functools.partial(update_kernel, pieces), grid=(1,), out_s...  96.9 us
    ppermute x7, waiting for transfers between devices, body(): lax.ppermute(rotated[shift], 'lon', [(i, (i + shift) % parts) for i in ra...  59 us
    all_to_all x3, waiting for transfers between devices, body(): lax.all_to_all(done.reshape(parts, group, levels, rows, clon), 'lon', spl...  56.3 us
    ppermute x7, starting transfers between devices, body(): lax.ppermute(rotated[shift], 'lon', [(i, (i + shift) % parts) for i in ra...  38.6 us
    pallas_call x1, Pallas kernels, body(): pl.pallas_call(pick_kernel, grid_spec=pltpu.PrefetchScalarGridSpec(num_sc...  20.6 us
    all_gather x1, blocking collectives, body(): places = lax.all_gather(places, 'lon', axis=0, tiled=True)  13.4 us
    all_to_all x3, starting transfers between devices, body(): lax.all_to_all(done.reshape(parts, group, levels, rows, clon), 'lon', spl...  13.1 us
    ppermute x4, waiting for transfers between devices, extended(): lax.ppermute(lax.slice_in_dim(block, block.shape[dim] - width, None, axis...  11.9 us
  transfers between devices with their start and end apart: 19, of which 13 were waited for; matrix products, arithmetic and copies ran while one was open for 3% of the time, Pallas kernels for 26%

profile of v3, /device:TPU:0, one launch (start us, length us, event | category | flops | bytes accessed | tf_op | source)
XLA Modules:
  0.0 358.6 jit_solution(8719024831851702934)
XLA Ops:
  0.0 0.5 broadcast.559
  0.5 1.3 reduce.25
  1.9 1.3 reduce.24
  3.4 13.4 %all-gather = s32[8,1,256]{2,1,0:T(1,128)S(1)} all-gather(s32[1,1,256]{2,1,0:T(1,128)S(1)} %add_bitcast_fusion), channel_id=1, replica_groups=mesh['lat'=4,'lon'=8] {'lon'}, dimensions={0}, use_global_device_ids=true | all-gather | bytes 9216 | tf_op jit(solution)/shard_map/all_gather | solution.py:111
  16.8 8.0 %fusion.38 = (f32[8,10,2,64,128]{4,3,2,1,0:T(8,128)}, f32[10,2,64,8,128]{4,2,1,0,3:T(8,128)}) fusion(f32[10,2,64,1024]{3,2,1,0:T(8,128)} %param.7), kind=kLoop, calls=%fused_computation.145 | loop fusion | bytes 15728640 | tf_op jit(solution)/shard_map/transpose | solution.py:113
  24.8 4.7 %all-to-all-start = ((f32[8,10,2,64,128]{4,3,2,1,0:T(8,128)}), f32[8,10,2,64,128]{4,3,2,1,0:T(8,128)}, u32[]{:S(2)}, u32[]{:S(2)}) async-start(f32[8,10,2,64,128]{4,3,2,1,0:T(8,128)} %get-tuple-element.26), calls=%async_computation | async-start | bytes 10485760 | tf_op jit(solution)/shard_map/all_to_all | solution.py:114
  29.5 2.5 copy-done
  32.0 20.6 %shard_map.73 = f32[8,20,128]{2,1,0:T(8,128)S(1)} custom-call(s32[8,128]{1,0:T(8,128)S(1)} %get-tuple-element.45.rows_ref, s32[8,128]{1,0:T(8,128)S(1)} %get-tuple-element.44.cols_ref, f32[10240,128]{1,0:T(8,128)S(1)} %bitcast.163), custom_call_target="tpu_custom_call" | custom-call | tf_op jit(solution)/shard_map/pallas_call | solution.py:117
  52.6 0.4 collective-permute-start.6
  53.1 1.7 collective-permute-start.5
  54.7 2.2 collective-permute-start.4
  57.0 1.4 collective-permute-start.3
  58.4 0.8 collective-permute-start
  59.3 0.6 fusion.40
  60.0 0.1 copy.37
  60.2 55.7 %collective-permute-done = f32[20,128]{1,0:T(8,128)S(1)} collective-permute-done((f32[20,128]{1,0:T(8,128)S(1)}, f32[20,128]{1,0:T(8,128)S(1)}, u32[]{:S(2)}, u32[]{:S(2)}) %collective-permute-start) | collective-permute-done | bytes 10272 | tf_op jit(solution)/shard_map/ppermute | solution.py:131
  115.8 3.5 collective-permute-start.1
  119.3 1.4 collective-permute-done.1
  120.7 28.5 %collective-permute-start.2 = (f32[20,128]{1,0:T(8,128)S(1)}, f32[20,128]{1,0:T(8,128)S(1)}, u32[]{:S(2)}, u32[]{:S(2)}) collective-permute-start(f32[20,128]{1,0:T(8,128)S(1)} %get-tuple-element.40), channel_id=1, source_target_pairs={{0,5},{1,6},{2,7},{3,0},{4,1},{5,2},{6,3},{7,4},{8,13},{9,14},{10,... | collective-permute-start | bytes 30728 | tf_op jit(solution)/shard_map/ppermute | solution.py:131
  149.3 1.9 collective-permute-done.2
  151.4 0.2 fusion.29
  151.7 0.7 fusion.34
  152.5 2.5 collective-permute-start.8
  155.1 1.5 collective-permute-done.8
  156.6 3.5 collective-permute-done.7
  160.2 0.5 collective-permute-start.9
  160.8 1.6 collective-permute-done.10
  162.4 4.5 %collective-permute-done.9 = f32[84,3,1,64]{0,3,2,1:T(8,128)S(1)} collective-permute-done((f32[84,3,1,64]{0,3,2,1:T(8,128)S(1)}, f32[84,3,1,64]{0,3,2,1:T(8,128)S(1)}, u32[]{:S(2)}, u32[]{:S(2)}) %collective-permute-start.9) | collective-permute-done | bytes 64544 | tf_op jit(solution)/shard_map/ppermute | solution.py:20
  167.0 0.7 slice_reduce_fusion.6
  168.0 0.2 copy.33
  168.2 0.4 select_select_fusion
  168.5 0.5 fusion.12
  169.1 0.4 fusion.24
  169.5 0.2 fusion.31
  169.7 0.2 multiply_reduce_fusion.1
  169.9 0.7 fusion.36
  170.8 0.1 concatenate.49
  170.9 2.0 collective-permute-start.11
  173.1 0.2 maximum_bitcast_fusion
  173.3 1.6 collective-permute-done.12
  174.8 1.0 collective-permute-done.11
  175.9 0.5 collective-permute-start.13
  176.4 2.5 collective-permute-done.14
  178.9 2.9 collective-permute-done.13
  181.8 0.7 slice_reduce_fusion.1
  182.8 0.2 copy.39
  183.1 0.2 maximum_bitcast_fusion.1
  183.4 0.1 pad_maximum_fusion.2.prior_ref
  183.5 0.4 fusion.3
  184.0 0.1 stack_broadcast_in_dim.17
  184.2 0.1 stack_broadcast_in_dim.15
  184.4 22.8 %shard_map.76 = f32[160,16,128]{2,1,0:T(8,128)} custom-call(f32[2,576,128]{2,1,0:T(8,128)S(1)} %maximum_subtract_fusion.lat_ref, f32[2,576,128]{2,1,0:T(8,128)S(1)} %pad_maximum_fusion.1.dx2_ref, bf16[2,576,240]{2,1,0:T(8,128)(2,1)S(1)} %pad_maximum_fusion.2.prior_ref, bf16[2,160,576]{2,1,0:T(8,128)(2,1)S(1)} %pad_maximum_fusion.3.coef_ref, ...), custom_call_target="tpu_custom_call" | custom-call | flops 32212254720 | bytes 8388608 | tf_op jit(solution)/shard_map/pallas_call | solution.py:201
  207.1 3.6 all-to-all-start.3
  210.7 39.8 %shard_map.75 = f32[160,24,128]{2,1,0:T(8,128)} custom-call(f32[2,576,128]{2,1,0:T(8,128)S(1)} %maximum_subtract_fusion.lat_ref, f32[2,576,128]{2,1,0:T(8,128)S(1)} %pad_maximum_fusion.1.dx2_ref, bf16[2,576,240]{2,1,0:T(8,128)(2,1)S(1)} %pad_maximum_fusion.2.prior_ref, bf16[2,160,576]{2,1,0:T(8,128)(2,1)S(1)} %pad_maximum_fusion.3.coef_ref, ...), custom_call_target="tpu_custom_call" | custom-call | flops 72477573120 | bytes 8388608 | tf_op jit(solution)/shard_map/pallas_call | solution.py:201
  250.5 1.1 copy-done.1
  251.6 5.0 %all-to-all-start.2 = ((f32[8,10,2,24,128]{4,3,2,1,0:T(8,128)}), f32[8,10,2,24,128]{4,3,2,1,0:T(8,128)}, u32[]{:S(2)}, u32[]{:S(2)}) async-start(f32[8,10,2,24,128]{4,3,2,1,0:T(8,128)} %bitcast.52), calls=%async_computation.2 | async-start | bytes 3932160 | tf_op jit(solution)/shard_map/all_to_all | solution.py:211
  256.6 34.4 %shard_map.74 = f32[160,24,128]{2,1,0:T(8,128)} custom-call(f32[2,576,128]{2,1,0:T(8,128)S(1)} %maximum_subtract_fusion.lat_ref, f32[2,576,128]{2,1,0:T(8,128)S(1)} %pad_maximum_fusion.1.dx2_ref, bf16[2,576,240]{2,1,0:T(8,128)(2,1)S(1)} %pad_maximum_fusion.2.prior_ref, bf16[2,160,576]{2,1,0:T(8,128)(2,1)S(1)} %pad_maximum_fusion.3.coef_ref, ...), custom_call_target="tpu_custom_call" | custom-call | flops 56371445760 | bytes 8388608 | tf_op jit(solution)/shard_map/pallas_call | solution.py:201
  291.0 12.0 %all-to-all-done.2 = f32[8,10,2,24,128]{4,3,2,1,0:T(8,128)} async-done(((f32[8,10,2,24,128]{4,3,2,1,0:T(8,128)}), f32[8,10,2,24,128]{4,3,2,1,0:T(8,128)}, u32[]{:S(2)}, u32[]{:S(2)}) %all-to-all-start.2) | async-done | bytes 1966112 | tf_op jit(solution)/shard_map/all_to_all | solution.py:211
  303.0 4.5 %all-to-all-start.1 = ((f32[8,10,2,24,128]{4,3,2,1,0:T(8,128)}), f32[8,10,2,24,128]{4,3,2,1,0:T(8,128)}, u32[]{:S(2)}, u32[]{:S(2)}) async-start(f32[8,10,2,24,128]{4,3,2,1,0:T(8,128)} %bitcast.50), calls=%async_computation.1 | async-start | bytes 3932160 | tf_op jit(solution)/shard_map/all_to_all | solution.py:211
  307.5 0.2 copy_bitcast_fusion.3
  307.6 1.8 copy_bitcast_fusion.1
  309.4 44.3 %all-to-all-done.1 = f32[8,10,2,24,128]{4,3,2,1,0:T(8,128)} async-done(((f32[8,10,2,24,128]{4,3,2,1,0:T(8,128)}), f32[8,10,2,24,128]{4,3,2,1,0:T(8,128)}, u32[]{:S(2)}, u32[]{:S(2)}) %all-to-all-start.1) | async-done | bytes 1966112 | tf_op jit(solution)/shard_map/all_to_all | solution.py:211
  353.7 1.8 copy_bitcast_fusion.2
  355.5 3.0 pad_maximum_fusion
  (87 shorter events, 2.3 us)
Async XLA Ops:
  24.8 159.6 %all-to-all-start = ((f32[8,10,2,64,128]{4,3,2,1,0:T(8,128)}), f32[8,10,2,64,128]{4,3,2,1,0:T(8,128)}, u32[]{:S(2)}, u32[]{:S(2)}) async-start(f32[8,10,2,64,128]{4,3,2,1,0:T(8,128)} %get-tuple-element.26), calls=%async_computation | async-start | bytes 10485760 | tf_op jit(solution)/shard_map/all_to_all | solution.py:114
  29.5 2.5 copy-start
  31.9 27.3 %copy-start.6 = (s32[2,1,1]{0,2,1:T(1,128)S(1)}, s32[2,1,1]{0,2,1:T(1,128)}, u32[]{:S(2)}) copy-start(s32[2,1,1]{0,2,1:T(1,128)} %param.13) | copy-start | bytes 28
  31.9 28.0 %copy-start.5 = (f32[2,1,1,2,64]{4,3,2,1,0:T(2,128)S(1)}, f32[2,1,1,2,64]{4,3,2,1,0:T(2,128)}, u32[]{:S(2)}) copy-start(f32[2,1,1,2,64]{4,3,2,1,0:T(2,128)} %param.12) | copy-start | bytes 3076
  32.0 28.0 %copy-start.3 = (s32[2,1,1,64]{3,2,1,0:T(1,128)S(1)}, s32[2,1,1,64]{3,2,1,0:T(1,128)}, u32[]{:S(2)}) copy-start(s32[2,1,1,64]{3,2,1,0:T(1,128)} %param.9) | copy-start | bytes 1540
  32.0 28.0 %copy-start.4 = (s32[2,1,1,64]{3,2,1,0:T(1,128)S(1)}, s32[2,1,1,64]{3,2,1,0:T(1,128)}, u32[]{:S(2)}) copy-start(s32[2,1,1,64]{3,2,1,0:T(1,128)} %param.8) | copy-start | bytes 1540
  32.0 119.7 %copy-start.7 = (f32[2,1,1,64]{3,2,1,0:T(1,128)S(1)}, f32[2,1,1,64]{3,2,1,0:T(1,128)}, u32[]{:S(2)}) copy-start(f32[2,1,1,64]{3,2,1,0:T(1,128)} %param.11) | copy-start | bytes 1540
  32.0 119.7 %copy-start.8 = (f32[2,1,1,64]{3,2,1,0:T(1,128)S(1)}, f32[2,1,1,64]{3,2,1,0:T(1,128)}, u32[]{:S(2)}) copy-start(f32[2,1,1,64]{3,2,1,0:T(1,128)} %param.10) | copy-start | bytes 1540
  52.6 98.6 %collective-permute-start.6 = (f32[20,128]{1,0:T(8,128)S(1)}, f32[20,128]{1,0:T(8,128)S(1)}, u32[]{:S(2)}, u32[]{:S(2)}) collective-permute-start(f32[20,128]{1,0:T(8,128)S(1)} %get-tuple-element.36), channel_id=1, source_target_pairs={{0,1},{1,2},{2,3},{3,4},{4,5},{5,6},{6,7},{7,0},{8,9},{9,10},{10,1... | collective-permute-start | bytes 30728 | tf_op jit(solution)/shard_map/ppermute | solution.py:131
  53.1 98.1 %collective-permute-start.5 = (f32[20,128]{1,0:T(8,128)S(1)}, f32[20,128]{1,0:T(8,128)S(1)}, u32[]{:S(2)}, u32[]{:S(2)}) collective-permute-start(f32[20,128]{1,0:T(8,128)S(1)} %get-tuple-element.37), channel_id=1, source_target_pairs={{0,2},{1,3},{2,4},{3,5},{4,6},{5,7},{6,0},{7,1},{8,10},{9,11},{10,... | collective-permute-start | bytes 30728 | tf_op jit(solution)/shard_map/ppermute | solution.py:131
  54.7 96.5 %collective-permute-start.4 = (f32[20,128]{1,0:T(8,128)S(1)}, f32[20,128]{1,0:T(8,128)S(1)}, u32[]{:S(2)}, u32[]{:S(2)}) collective-permute-start(f32[20,128]{1,0:T(8,128)S(1)} %get-tuple-element.38), channel_id=1, source_target_pairs={{0,3},{1,4},{2,5},{3,6},{4,7},{5,0},{6,1},{7,2},{8,11},{9,12},{10,... | collective-permute-start | bytes 30728 | tf_op jit(solution)/shard_map/ppermute | solution.py:131
  57.0 94.2 %collective-permute-start.3 = (f32[20,128]{1,0:T(8,128)S(1)}, f32[20,128]{1,0:T(8,128)S(1)}, u32[]{:S(2)}, u32[]{:S(2)}) collective-permute-start(f32[20,128]{1,0:T(8,128)S(1)} %get-tuple-element.39), channel_id=1, source_target_pairs={{0,4},{1,5},{2,6},{3,7},{4,0},{5,1},{6,2},{7,3},{8,12},{9,13},{10,... | collective-permute-start | bytes 30728 | tf_op jit(solution)/shard_map/ppermute | solution.py:131
  58.4 57.4 %collective-permute-start = (f32[20,128]{1,0:T(8,128)S(1)}, f32[20,128]{1,0:T(8,128)S(1)}, u32[]{:S(2)}, u32[]{:S(2)}) collective-permute-start(f32[20,128]{1,0:T(8,128)S(1)} %get-tuple-element.42), channel_id=1, source_target_pairs={{0,7},{1,0},{2,1},{3,2},{4,3},{5,4},{6,5},{7,6},{8,15},{9,8},{10,9... | collective-permute-start | bytes 30728 | tf_op jit(solution)/shard_map/ppermute | solution.py:131
  115.8 4.9 %collective-permute-start.1 = (f32[20,128]{1,0:T(8,128)S(1)}, f32[20,128]{1,0:T(8,128)S(1)}, u32[]{:S(2)}, u32[]{:S(2)}) collective-permute-start(f32[20,128]{1,0:T(8,128)S(1)} %get-tuple-element.41), channel_id=1, source_target_pairs={{0,6},{1,7},{2,0},{3,1},{4,2},{5,3},{6,4},{7,5},{8,14},{9,15},{10,... | collective-permute-start | bytes 30728 | tf_op jit(solution)/shard_map/ppermute | solution.py:131
  120.7 30.5 %collective-permute-start.2 = (f32[20,128]{1,0:T(8,128)S(1)}, f32[20,128]{1,0:T(8,128)S(1)}, u32[]{:S(2)}, u32[]{:S(2)}) collective-permute-start(f32[20,128]{1,0:T(8,128)S(1)} %get-tuple-element.40), channel_id=1, source_target_pairs={{0,5},{1,6},{2,7},{3,0},{4,1},{5,2},{6,3},{7,4},{8,13},{9,14},{10,... | collective-permute-start | bytes 30728 | tf_op jit(solution)/shard_map/ppermute | solution.py:131
  152.5 4.1 %collective-permute-start.8 = (f32[84,1,1,64]{0,3,2,1:T(8,128)S(1)}, f32[84,1,1,64]{0,3,2,1:T(8,128)S(1)}, u32[]{:S(2)}, u32[]{:S(2)}) collective-permute-start(f32[84,1,1,64]{0,3,2,1:T(8,128)S(1)} %bitcast.171), channel_id=1, source_target_pairs={{8,0},{16,8},{24,16},{0,24},{9,1},{17,9},{25,17},{1,25},{10,2},{18... | collective-permute-start | bytes 64520 | tf_op jit(solution)/shard_map/ppermute | solution.py:23
  155.0 5.1 %collective-permute-start.7 = (f32[84,1,1,64]{0,3,2,1:T(8,128)S(1)}, f32[84,1,1,64]{0,3,2,1:T(8,128)S(1)}, u32[]{:S(2)}, u32[]{:S(2)}) collective-permute-start(f32[84,1,1,64]{0,3,2,1:T(8,128)S(1)} %bitcast.172), channel_id=1, source_target_pairs={{0,8},{8,16},{16,24},{24,0},{1,9},{9,17},{17,25},{25,1},{2,10},{10... | collective-permute-start | bytes 64520 | tf_op jit(solution)/shard_map/ppermute | solution.py:20
  160.1 2.3 collective-permute-start.10
  160.2 6.8 %collective-permute-start.9 = (f32[84,3,1,64]{0,3,2,1:T(8,128)S(1)}, f32[84,3,1,64]{0,3,2,1:T(8,128)S(1)}, u32[]{:S(2)}, u32[]{:S(2)}) collective-permute-start(f32[84,3,1,64]{0,3,2,1:T(8,128)S(1)} %pad_maximum_fusion.6), channel_id=1, source_target_pairs={{0,1},{1,2},{2,3},{3,4},{4,5},{5,6},{6,7},{7,0},{8,9},{9,10},{10,1... | collective-permute-start | bytes 193544 | tf_op jit(solution)/shard_map/ppermute | solution.py:20
  170.9 4.0 %collective-permute-start.12 = (f32[84,1,1,64]{0,3,2,1:T(8,128)S(1)}, f32[84,1,1,64]{0,3,2,1:T(8,128)S(1)}, u32[]{:S(2)}, u32[]{:S(2)}) collective-permute-start(f32[84,1,1,64]{0,3,2,1:T(8,128)S(1)} %bitcast.175), channel_id=1, source_target_pairs={{8,0},{16,8},{24,16},{0,24},{9,1},{17,9},{25,17},{1,25},{10,2},{18... | collective-permute-start | bytes 64520 | tf_op jit(solution)/shard_map/ppermute | solution.py:23
  170.9 4.9 %collective-permute-start.11 = (f32[84,1,1,64]{0,3,2,1:T(8,128)S(1)}, f32[84,1,1,64]{0,3,2,1:T(8,128)S(1)}, u32[]{:S(2)}, u32[]{:S(2)}) collective-permute-start(f32[84,1,1,64]{0,3,2,1:T(8,128)S(1)} %bitcast.176), channel_id=1, source_target_pairs={{0,8},{8,16},{16,24},{24,0},{1,9},{9,17},{17,25},{25,1},{2,10},{10... | collective-permute-start | bytes 64520 | tf_op jit(solution)/shard_map/ppermute | solution.py:20
  175.8 3.1 collective-permute-start.14
  175.9 5.9 %collective-permute-start.13 = (f32[84,3,1,64]{0,3,2,1:T(8,128)S(1)}, f32[84,3,1,64]{0,3,2,1:T(8,128)S(1)}, u32[]{:S(2)}, u32[]{:S(2)}) collective-permute-start(f32[84,3,1,64]{0,3,2,1:T(8,128)S(1)} %pad_maximum_fusion.7), channel_id=1, source_target_pairs={{0,1},{1,2},{2,3},{3,4},{4,5},{5,6},{6,7},{7,0},{8,9},{9,10},{10,1... | collective-permute-start | bytes 193544 | tf_op jit(solution)/shard_map/ppermute | solution.py:20
  207.1 43.4 %all-to-all-start.3 = ((f32[8,10,2,16,128]{4,3,2,1,0:T(8,128)}), f32[8,10,2,16,128]{4,3,2,1,0:T(8,128)S(1)}, u32[]{:S(2)}, u32[]{:S(2)}) async-start(f32[8,10,2,16,128]{4,3,2,1,0:T(8,128)} %bitcast.54), calls=%async_computation.3 | async-start | bytes 2621440 | tf_op jit(solution)/shard_map/all_to_all | solution.py:211
  250.5 1.1 copy-start.1
  251.6 51.4 %all-to-all-start.2 = ((f32[8,10,2,24,128]{4,3,2,1,0:T(8,128)}), f32[8,10,2,24,128]{4,3,2,1,0:T(8,128)}, u32[]{:S(2)}, u32[]{:S(2)}) async-start(f32[8,10,2,24,128]{4,3,2,1,0:T(8,128)} %bitcast.52), calls=%async_computation.2 | async-start | bytes 3932160 | tf_op jit(solution)/shard_map/all_to_all | solution.py:211
  303.0 4.5 %copy-start.2 = (f32[8,10,2,16,128]{4,3,2,1,0:T(8,128)S(1)}, f32[8,10,2,16,128]{4,3,2,1,0:T(8,128)}, u32[]{:S(2)}) copy-start(f32[8,10,2,16,128]{4,3,2,1,0:T(8,128)} %copy-done.1) | copy-start | bytes 3932164
  303.0 50.7 %all-to-all-start.1 = ((f32[8,10,2,24,128]{4,3,2,1,0:T(8,128)}), f32[8,10,2,24,128]{4,3,2,1,0:T(8,128)}, u32[]{:S(2)}, u32[]{:S(2)}) async-start(f32[8,10,2,24,128]{4,3,2,1,0:T(8,128)} %bitcast.50), calls=%async_computation.1 | async-start | bytes 3932160 | tf_op jit(solution)/shard_map/all_to_all | solution.py:211
